TPU v7x, 32 devices: a whole 2x2x4 slice. The times are simulated.
32 devices in a mesh: shard: 4 (over z), ctx: 4 (over y, x), tp: 2 (over core).
Axes of the slice: x: 2, y: 2, z: 4, core: 2. Of those that a mesh axis runs over, the one named last changes fastest.
Arguments:
- tokens: bfloat16 [4, 4096, 1024], P('shard', 'ctx'), may hold values from -6 to 6
- lengths: int32 [4], P('shard'), may hold values from 1024 to 4096, as said below
- routes: int32 [4, 4096, 1], P('shard', 'ctx'), may hold values from 0 to 15
- query_key_value_weight: bfloat16 [3, 1024, 1024], P(None, ('shard', 'ctx'), 'tp'), may hold values from -0.1875 to 0.1875
- context_blend_linear_map: bfloat16 [1024, 1024], P(('shard', 'ctx'), 'tp'), may hold values from -3 to 3
- router: bfloat16 [1024, 16], P(('shard', 'ctx')), may hold values from -0.09375 to 0.09375
- gain_one: bfloat16 [1024], P(('shard', 'ctx')), may hold values from 0.5 to 1.5
- gain_two: bfloat16 [1024], P(('shard', 'ctx')), may hold values from 0.5 to 1.5
- w_in: bfloat16 [16, 1024, 4096], P(('shard', 'ctx'), None, 'tp'), may hold values from -0.1875 to 0.1875
- w_out: bfloat16 [16, 4096, 1024], P(('shard', 'ctx'), 'tp'), may hold values from -1.5 to 1.5
- cotangent: bfloat16 [4, 4096, 1024], P('shard', 'ctx'), may hold values from -6 to 6
Outputs:
- output: bfloat16 [4, 4096, 1024], P('shard', 'ctx')
- grad_tokens: float32 [4, 4096, 1024], P('shard', 'ctx')
- grad_w_qkv: float32 [3, 1024, 1024], P(None, ('shard', 'ctx'), 'tp')
- grad_attn_proj: float32 [1024, 1024], P(('shard', 'ctx'), 'tp')
- grad_router: float32 [1024, 16], P(('shard', 'ctx'))
- grad_gain_one: float32 [1024], P(('shard', 'ctx'))
- grad_gain_two: float32 [1024], P(('shard', 'ctx'))
- grad_w_in: float32 [16, 1024, 4096], P(('shard', 'ctx'), None, 'tp')
- grad_w_out: float32 [16, 4096, 1024], P(('shard', 'ctx'), 'tp')
Inputs may be any that keep to these rules, and one draw needn't show every extreme that they name: `lengths`: at least one slot has all 4096 positions used.
All inputs are finite; a program needn't handle non-finite values.
Results may differ from a plain program's by a relative error of at most 0.03.
Values may be sent and summed in bfloat16 or wider, within the bound.
A program may use at most 256 MiB of HBM per device.

v0:
```python
import math

import jax
import jax.numpy as jnp
from jax import lax
from jax.sharding import PartitionSpec as P

HEAD_DIM = 64


epsilon = 1e-05
masked_score = -1e30
key_block = 512


def norm_parts(values, gain):
    center = values - jnp.mean(values, axis=-1, keepdims=True)
    multiplier_coefficient = lax.rsqrt(jnp.mean(center * center, axis=-1, keepdims=True) + epsilon)
    normed = center * multiplier_coefficient
    return (normed * gain, normed, multiplier_coefficient)


def norm_back(grad, normed, multiplier_coefficient, gain):
    scaled = grad * gain
    inner = (
        scaled
        - jnp.mean(scaled, axis=-1, keepdims=True)
        - normed * jnp.mean(scaled * normed, axis=-1, keepdims=True)
    )
    return (inner * multiplier_coefficient, jnp.sum(grad * normed, axis=0))


def score_block(query, block, begin, query_places, lengths, heads):
    slots, block_len, twice = block.shape
    half = twice // 2
    keys = block[:, :, :half].reshape(slots, block_len, heads, HEAD_DIM)
    values = block[:, :, half:].reshape(slots, block_len, heads, HEAD_DIM)
    key_places = begin + jnp.arange(block_len, dtype=jnp.int32)
    allowed = (key_places[None, None, :] <= query_places[None, :, None]) & (
        key_places[None, None, :] < lengths[:, None, None]
    )
    scores = jnp.einsum(
        "sqhd,skhd->sqhk", query, keys, preferred_element_type=jnp.float32
    ) * HEAD_DIM ** (-0.5)
    return (keys, values, allowed[:, :, None, :], scores)


def contract_rows(left, right):
    return lax.dot_general(
        left, right, (((0,), (0,)), ((), ())), preferred_element_type=jnp.float32
    )


def contract_cols(left, right):
    return lax.dot_general(
        left, right, (((1,), (1,)), ((), ())), preferred_element_type=jnp.float32
    )


def local(
    tokens,
    lengths,
    routes,
    query_key_value_weight,
    context_blend_linear_map,
    router,
    gain_one,
    gain_two,
    w_in,
    w_out,
    cotangent,
):
    slots, local_len, width = tokens.shape
    count = slots * local_len
    head_width = query_key_value_weight.shape[2]
    heads = head_width // HEAD_DIM
    experts = router.shape[1]
    capacity = max(2, (5 * count + 4 * experts - 1) // (4 * experts))
    scale = HEAD_DIM ** (-0.5)
    ctx_rank = lax.axis_index("ctx")
    query_places = ctx_rank * local_len + jnp.arange(local_len, dtype=jnp.int32)
    full_qkv, full_proj, full_router, full_one, full_two = (
        lax.all_gather(query_key_value_weight, ("shard", "ctx"), axis=1, tiled=True),
        lax.all_gather(context_blend_linear_map, ("shard", "ctx"), axis=0, tiled=True),
        lax.all_gather(router, ("shard", "ctx"), axis=0, tiled=True),
        lax.all_gather(gain_one, ("shard", "ctx"), axis=0, tiled=True),
        lax.all_gather(gain_two, ("shard", "ctx"), axis=0, tiled=True),
    )
    scale_one = full_one.astype(jnp.float32)
    scale_two = full_two.astype(jnp.float32)
    inputs = tokens.astype(jnp.float32).reshape(count, width)
    normed_one, unit_one, inverse_one = norm_parts(inputs, scale_one)
    first_part = normed_one.astype(jnp.bfloat16)
    projected_rows = jnp.einsum(
        "td,kdf->tkf", first_part, full_qkv, preferred_element_type=jnp.float32
    ).astype(jnp.bfloat16)
    query = projected_rows[:, 0].reshape(slots, local_len, heads, HEAD_DIM)
    pairs = projected_rows[:, 1:].reshape(slots, local_len, 2 * head_width)
    start_state = (
        jnp.full((slots, local_len, heads), masked_score, jnp.float32),
        jnp.zeros((slots, local_len, heads), jnp.float32),
        jnp.zeros((slots, local_len, heads, HEAD_DIM), jnp.float32),
    )
    piece = lax.all_gather(pairs, "ctx", axis=1, tiled=True)
    piece_len = piece.shape[1]
    step_size = math.gcd(piece_len, key_block)

    def inner(number, state):
        top, total, accum = state
        offset = number * step_size
        block = lax.dynamic_slice_in_dim(piece, offset, step_size, 1)
        keys, values, allowed, scores = score_block(
            query, block, offset, query_places, lengths, heads
        )
        scores = jnp.where(allowed, scores, masked_score)
        new_top = jnp.maximum(top, jnp.max(scores, axis=-1))
        factor = jnp.exp(top - new_top)
        weights = jnp.where(allowed, jnp.exp(scores - new_top[..., None]), 0.0)
        total = total * factor + jnp.sum(weights, axis=-1)
        accum = accum * factor[..., None] + jnp.einsum(
            "sqhk,skhd->sqhd",
            weights.astype(jnp.bfloat16),
            values,
            preferred_element_type=jnp.float32,
        )
        return (new_top, total, accum)

    top, total, accum = lax.fori_loop(0, piece_len // step_size, inner, start_state)
    log_total = top + jnp.log(total)
    blended_layer_yield = (accum / total[..., None]).astype(jnp.bfloat16)
    mixed_rows = blended_layer_yield.reshape(count, head_width)
    partial_branch = jnp.einsum(
        "tf,df->td", mixed_rows, full_proj, preferred_element_type=jnp.float32
    )
    expert_path_yield = lax.psum(partial_branch.astype(jnp.bfloat16), "tp").astype(jnp.float32)
    middle = inputs + expert_path_yield
    normed_two, unit_two, inverse_two = norm_parts(middle, scale_two)
    second_part = normed_two.astype(jnp.bfloat16)
    router_logits = jnp.dot(second_part, full_router, preferred_element_type=jnp.float32)
    probs = jax.nn.softmax(router_logits, axis=-1)
    route = routes.reshape(count)
    valid = (query_places[None, :] < lengths[:, None]).reshape(count)
    expert_ids = jnp.arange(experts, dtype=jnp.int32)
    route_hot = route[:, None] == expert_ids[None, :]
    gate = jnp.sum(jnp.where(route_hot, probs, 0.0), axis=1)
    counted = (route_hot & valid[:, None]).astype(jnp.int32)
    earlier = jnp.cumsum(counted, axis=0) - counted
    place = jnp.sum(earlier * counted, axis=1)
    kept = valid & (place < capacity)
    target = jnp.where(kept, route * capacity + place, experts * capacity)
    send = (
        jnp.zeros((experts * capacity + 1, width), jnp.bfloat16)
        .at[target]
        .set(second_part)[:-1]
        .reshape(experts, capacity, width)
    )
    arrived_here = lax.all_to_all(send, ("shard", "ctx"), split_axis=0, concat_axis=0, tiled=True)
    sources, items, _ = arrived_here.shape
    arrived_rows = arrived_here.reshape(sources * items, width)
    pre = jnp.dot(arrived_rows, w_in[0], preferred_element_type=jnp.float32)
    hidden = jax.nn.gelu(pre).astype(jnp.bfloat16)
    partial_out = jnp.dot(hidden, w_out[0], preferred_element_type=jnp.float32)
    summed = lax.psum(partial_out.astype(jnp.bfloat16), "tp")
    going_back = lax.all_to_all(
        summed.reshape(sources, items, width),
        ("shard", "ctx"),
        split_axis=0,
        concat_axis=0,
        tiled=True,
    )
    pre_act = pre.reshape(sources, items, pre.shape[1])
    fetched = jnp.concatenate(
        [going_back.reshape(experts * capacity, width), jnp.zeros((1, width), jnp.bfloat16)], axis=0
    )[target]
    fetched_value = fetched.astype(jnp.float32)
    kept_value = kept.astype(jnp.float32)
    valid_value = valid.astype(jnp.float32)
    weighted_gate = kept_value * gate
    moe = weighted_gate[:, None] * fetched_value
    output = (
        (valid_value[:, None] * (middle + moe))
        .astype(jnp.bfloat16)
        .reshape(slots, local_len, width)
    )
    grad_out = valid_value[:, None] * cotangent.astype(jnp.float32).reshape(count, width)
    grad_fetched = (weighted_gate[:, None] * grad_out).astype(jnp.bfloat16)
    grad_send = (
        jnp.zeros((experts * capacity + 1, width), jnp.bfloat16)
        .at[target]
        .set(grad_fetched)[:-1]
        .reshape(experts, capacity, width)
    )
    grad_arrived = lax.all_to_all(
        grad_send, ("shard", "ctx"), split_axis=0, concat_axis=0, tiled=True
    )
    arrived_rows = arrived_here.reshape(-1, width)
    grad_rows = grad_arrived.reshape(-1, width)
    pre_rows = pre_act.reshape(arrived_rows.shape[0], pre_act.shape[2])
    hidden_rows = jax.nn.gelu(pre_rows).astype(jnp.bfloat16)
    grad_w_out = contract_rows(hidden_rows, grad_rows)[None]
    grad_hidden = contract_cols(grad_rows, w_out[0])
    unused_value, gelu_back = jax.vjp(jax.nn.gelu, pre_rows)
    grad_pre = gelu_back(grad_hidden)[0].astype(jnp.bfloat16)
    grad_w_in = contract_rows(arrived_rows, grad_pre)[None]
    partial_grad = contract_cols(grad_pre, w_in[0])
    grad_dispatched = lax.psum(partial_grad.astype(jnp.bfloat16), "tp")
    grad_home = lax.all_to_all(
        grad_dispatched.reshape(arrived_here.shape),
        ("shard", "ctx"),
        split_axis=0,
        concat_axis=0,
        tiled=True,
    )
    grad_home_rows = jnp.concatenate(
        [grad_home.reshape(experts * capacity, width), jnp.zeros((1, width), jnp.bfloat16)], axis=0
    )[target].astype(jnp.float32)
    grad_gate = kept_value * jnp.sum(grad_out * fetched_value, axis=1)
    grad_logits = ((grad_gate * gate)[:, None] * (route_hot.astype(jnp.float32) - probs)).astype(
        jnp.bfloat16
    )
    grad_router = contract_rows(second_part, grad_logits)
    grad_second = grad_home_rows + contract_cols(grad_logits, full_router)
    lifted_two, grad_gain_two = norm_back(grad_second, unit_two, inverse_two, scale_two)
    grad_middle = grad_out + lifted_two
    grad_branch = grad_middle.astype(jnp.bfloat16)
    grad_proj = contract_rows(grad_branch, mixed_rows)
    grad_mixed = (
        jnp.dot(grad_branch, full_proj, preferred_element_type=jnp.float32)
        .astype(jnp.bfloat16)
        .reshape(slots, local_len, heads, HEAD_DIM)
    )
    delta = jnp.sum(
        grad_mixed.astype(jnp.float32) * blended_layer_yield.astype(jnp.float32), axis=-1
    )
    every_pair = lax.all_gather(pairs, "ctx", axis=1, tiled=True)
    piece_len = every_pair.shape[1]
    key_step_size = math.gcd(piece_len, key_block)

    def inner(number, state):
        grad_query, grad_piece = state
        offset = number * key_step_size
        block = lax.dynamic_slice_in_dim(every_pair, offset, key_step_size, 1)
        keys, values, allowed, scores = score_block(
            query, block, 0 + offset, query_places, lengths, heads
        )
        weights = jnp.where(allowed, jnp.exp(scores - log_total[..., None]), 0.0)
        grad_values = jnp.einsum(
            "sqhk,sqhd->skhd",
            weights.astype(jnp.bfloat16),
            grad_mixed,
            preferred_element_type=jnp.float32,
        )
        grad_weights = jnp.einsum(
            "sqhd,skhd->sqhk", grad_mixed, values, preferred_element_type=jnp.float32
        )
        grad_scores = (weights * (grad_weights - delta[..., None])).astype(jnp.bfloat16)
        grad_query = (
            grad_query
            + jnp.einsum("sqhk,skhd->sqhd", grad_scores, keys, preferred_element_type=jnp.float32)
            * scale
        )
        grad_keys = (
            jnp.einsum("sqhk,sqhd->skhd", grad_scores, query, preferred_element_type=jnp.float32)
            * scale
        )
        update = jnp.concatenate(
            [
                grad_keys.reshape(slots, key_step_size, head_width),
                grad_values.reshape(slots, key_step_size, head_width),
            ],
            axis=-1,
        )
        return (grad_query, lax.dynamic_update_slice_in_dim(grad_piece, update, offset, 1))

    state = (
        jnp.zeros((slots, local_len, heads, HEAD_DIM), jnp.float32),
        jnp.zeros((slots, piece_len, 2 * head_width), jnp.float32),
    )
    grad_query_total, grad_all_pairs = lax.fori_loop(0, piece_len // key_step_size, inner, state)
    grad_pairs = lax.psum_scatter(
        grad_all_pairs.astype(jnp.bfloat16), "ctx", scatter_dimension=1, tiled=True
    )
    grad_query_rows = grad_query_total.astype(jnp.bfloat16).reshape(count, 1, head_width)
    grad_pair_rows = grad_pairs.reshape(count, 2, head_width)
    grad_projected = jnp.concatenate([grad_query_rows, grad_pair_rows], axis=1)
    grad_qkv = jnp.einsum(
        "td,tkf->kdf", first_part, grad_projected, preferred_element_type=jnp.float32
    )
    partial_first = jnp.einsum(
        "tkf,kdf->td", grad_projected, full_qkv, preferred_element_type=jnp.float32
    )
    grad_first = lax.psum(partial_first.astype(jnp.bfloat16), "tp").astype(jnp.float32)
    lifted_one, grad_gain_one = norm_back(grad_first, unit_one, inverse_one, scale_one)
    grad_tokens = (grad_middle + lifted_one).reshape(slots, local_len, width)
    shard_qkv, shard_proj, shard_router, shard_one, shard_two = (
        lax.psum_scatter(grad_qkv, ("shard", "ctx"), scatter_dimension=1, tiled=True),
        lax.psum_scatter(grad_proj, ("shard", "ctx"), scatter_dimension=0, tiled=True),
        lax.psum_scatter(grad_router, ("shard", "ctx"), scatter_dimension=0, tiled=True),
        lax.psum_scatter(grad_gain_one, ("shard", "ctx"), scatter_dimension=0, tiled=True),
        lax.psum_scatter(grad_gain_two, ("shard", "ctx"), scatter_dimension=0, tiled=True),
    )
    return (
        output,
        grad_tokens,
        shard_qkv,
        shard_proj,
        shard_router,
        shard_one,
        shard_two,
        grad_w_in,
        grad_w_out,
    )


def solution(mesh):
    return jax.shard_map(
        local,
        mesh=mesh,
        in_specs=(
            P("shard", "ctx", None),
            P("shard"),
            P("shard", "ctx", None),
            P(None, ("shard", "ctx"), "tp"),
            P(("shard", "ctx"), "tp"),
            P(("shard", "ctx"), None),
            P(("shard", "ctx")),
            P(("shard", "ctx")),
            P(("shard", "ctx"), None, "tp"),
            P(("shard", "ctx"), "tp", None),
            P("shard", "ctx", None),
        ),
        out_specs=(
            P("shard", "ctx", None),
            P("shard", "ctx", None),
            P(None, ("shard", "ctx"), "tp"),
            P(("shard", "ctx"), "tp"),
            P(("shard", "ctx"), None),
            P(("shard", "ctx")),
            P(("shard", "ctx")),
            P(("shard", "ctx"), None, "tp"),
            P(("shard", "ctx"), "tp", None),
        ),
        check_vma=False,
    )
```

profile of v0, /device:TPU:0, one launch (start us, length us, event | category | flops | bytes accessed | tf_op | source)
XLA Modules:
  0.0 1555.2 jit_solution(8912347346169904644)
XLA Ops:
  11.6 43.8 %all-reduce.8 = (bf16[1024]{0:T(1024)(128)(2,1)S(1)}, bf16[1024]{0:T(1024)(128)(2,1)S(1)}) all-reduce(bf16[1024]{0:T(1024)(128)(2,1)S(1)} %dynamic-update-slice.1, bf16[1024]{0:T(1024)(128)(2,1)S(1)} %dynamic-update-slice), channel_id=1, replica_groups=mesh['shard'=4,'ctx'=4,'tp'=2] {'shard','ctx'}, use_global_device_ids=true, to_apply=%add.3 | all-reduce | flops 2048 | bytes 8192
  59.8 21.7 %all-gather.5.cloned.1.call-done = bf16[3,1024,512]{2,1,0:T(8,128)(2,1)} async-done(((bf16[3,64,512]{2,1,0:T(8,128)(2,1)}), bf16[3,1024,512]{2,1,0:T(8,128)(2,1)}) %all-gather.5.cloned.1.call-update) | async-done | bytes 3145744 | tf_op jit(solution)/shard_map/all_gather | solution.py:83
  93.5 83.6 %all-gather.7.cloned.1.call-done = bf16[1,4096,1024]{1,2,0:T(8,128)(2,1)} async-done(((bf16[1,1024,1024]{1,2,0:T(8,128)(2,1)}), bf16[1,4096,1024]{1,2,0:T(8,128)(2,1)}) %all-gather.7.cloned.1.call-update) | async-done | bytes 8388624 | tf_op jit(solution)/shard_map/all_gather | solution.py:104
  177.1 133.8 %while.34 = (s32[]{:T(128)}, f32[1,1024,8]{1,2,0:T(8,128)S(1)}, f32[1,1024,8]{1,2,0:T(8,128)S(1)}, f32[1,1024,8,64]{1,3,2,0:T(8,128)}, s32[1]{0:T(128)}, /*index...) while((s32[]{:T(128)}, f32[1,1024,8]{1,2,0:T(8,128)S(1)}, ...), condition=%wide.region_5.6_spmd.clone, body=%wide.region_2.5_spmd.clone.sunk | while | flops 1130940928 | bytes 61355232 | solution.py:128
  323.7 15.7 %all-reduce.15.cloned.1.call-done = bf16[1024,1024]{1,0:T(8,128)(2,1)} async-done(((bf16[1024,1024]{1,0:T(8,128)(2,1)}), bf16[1024,1024]{1,0:T(8,128)(2,1)}) %all-reduce.15.cloned.1.call-update) | async-done | bytes 2097168 | tf_op jit(solution)/shard_map/psum | solution.py:135
  363.2 78.6 %all-gather = bf16[16,64,16]{1,2,0:T(8,128)(2,1)S(1)} all-gather(bf16[1,64,16]{1,2,0:T(8,128)(2,1)S(1)} %bitcast.394), channel_id=1, replica_groups=mesh['shard'=4,'ctx'=4,'tp'=2] {'shard','ctx'}, dimensions={0}, use_global_device_ids=true | all-gather | bytes 34816 | tf_op jit(solution)/shard_map/all_gather | solution.py:85
  455.9 10.4 all-to-all-start.2
  486.7 26.5 %all-to-all-done.2 = bf16[16,80,1024]{2,1,0:T(8,128)(2,1)} async-done(((bf16[16,80,1024]{2,1,0:T(8,128)(2,1)}), bf16[16,80,1024]{2,1,0:T(8,128)(2,1)}, u32[]{:S(2)}, u32[]{:S(2)}) %all-to-all-start.2) | async-done | bytes 2621472 | tf_op jit(solution)/shard_map/all_to_all | solution.py:193
  513.1 15.5 fusion.50
  536.1 35.1 %all-reduce.21.cloned.1.call-done = (bf16[16,80,1024]{2,1,0:T(8,128)(2,1)}, bf16[16,80,1024]{2,1,0:T(8,128)(2,1)}) async-done(((bf16[16,80,1024]{2,1,0:T(8,128)(2,1)}, bf16[16,80,1024]{2,1,0:T(8,128)(2,1)}), (bf16[16,80,1024]{2,1,0:T(8,128)(2,1)}, bf16[16,80,1024]{2,1,0:T(8,128)(2,1)})) %all-reduce.21.cloned.1.call-update) | async-done | bytes 5242896 | tf_op jit(solution)/shard_map/psum | solution.py:163
  571.2 67.3 %all_to_all.20 = bf16[16,80,1024]{2,1,0:T(8,128)(2,1)} all-to-all(bf16[16,80,1024]{2,1,0:T(8,128)(2,1)} %get-tuple-element.465), channel_id=1, replica_groups=mesh['shard'=4,'ctx'=4,'tp'=2] {'shard','ctx'}, dimensions={0} | all-to-all | bytes 5242880 | tf_op jit(solution)/shard_map/all_to_all | solution.py:207
  654.7 39.5 %all-to-all-done.1 = bf16[16,80,1024]{2,1,0:T(8,128)(2,1)} async-done(((bf16[16,80,1024]{2,1,0:T(8,128)(2,1)}), bf16[16,80,1024]{2,1,0:T(8,128)(2,1)}, u32[]{:S(2)}, u32[]{:S(2)}) %all-to-all-start.1) | async-done | bytes 2621472 | tf_op jit(solution)/shard_map/all_to_all | solution.py:164
  723.9 284.3 %while.35 = (s32[]{:T(128)}, f32[1,1024,8,64]{1,3,2,0:T(8,128)}, bf16[1,4096,1024]{1,2,0:T(8,128)(2,1)}, bf16[1,4096,1024]{1,2,0:T(8,128)(2,1)}, s32[1]{0:T(128)...) while((s32[]{:T(128)}, f32[1,1024,8,64]{1,3,2,0:T(8,128)}, ...), condition=%wide.region_24.25_spmd.clone, body=%wide.region_23.24_spmd.clone.sunk | while | flops 2731543040 | bytes 109163824 | solution.py:279
  734.5 9.4 fusion.180
  743.9 9.5 fusion.179
  770.0 9.4 fusion.180
  779.4 9.5 fusion.179
  814.9 9.5 fusion.179
  850.4 9.5 fusion.179
  886.0 9.5 fusion.179
  921.5 9.5 fusion.179
  957.0 9.5 fusion.179
  992.5 9.5 fusion.179
  1015.0 86.0 %reduce-scatter.6.cloned.1.call-done = bf16[1,1024,1024]{1,2,0:T(8,128)(2,1)} async-done(((bf16[1,4096,1024]{1,2,0:T(8,128)(2,1)}), bf16[1,1024,1024]{1,2,0:T(8,128)(2,1)}) %reduce-scatter.6.cloned.1.call-update) | async-done | bytes 2097168 | tf_op jit(solution)/shard_map/reduce_scatter | solution.py:280
  1120.6 9.4 copy.53
  1136.1 11.1 convolution_bitcast_fusion.1
  1147.1 12.3 convolution_bitcast_fusion
  1159.4 21.4 %reduce-scatter.10.cloned.1.call-done = f32[64,16]{1,0:T(8,128)} async-done(((f32[1024,16]{1,0:T(8,128)}), f32[64,16]{1,0:T(8,128)}) %reduce-scatter.10.cloned.1.call-update) | async-done | bytes 4112
  1182.2 18.6 %all-reduce.17.cloned.1.call-done = bf16[1024,1024]{1,0:T(8,128)(2,1)} async-done(((bf16[1024,1024]{1,0:T(8,128)(2,1)}), bf16[1024,1024]{1,0:T(8,128)(2,1)}) %all-reduce.17.cloned.1.call-update) | async-done | bytes 2097168 | tf_op jit(solution)/shard_map/psum | solution.py:292
  1204.3 44.8 %all-reduce.7 = (f32[1024]{0:T(1024)S(1)}, f32[1024]{0:T(1024)S(1)}) all-reduce(f32[1024]{0:T(1024)S(1)} %get-tuple-element.420, f32[1024]{0:T(1024)S(1)} %copy-done.33), channel_id=6, replica_groups=mesh['shard'=4,'ctx'=4,'tp'=2] {'shard','ctx'}, use_global_device_ids=true, to_apply=%region_33.34.clone | all-reduce | flops 2048 | bytes 16384
  1255.3 209.6 %all-reduce.19.cloned.1.call-done = f32[3,1024,512]{2,0,1:T(4,128)} async-done(((f32[3,1024,512]{2,0,1:T(4,128)}), f32[3,1024,512]{2,0,1:T(4,128)}) %all-reduce.19.cloned.1.call-update) | async-done | bytes 6291472
  1466.8 81.3 %reduce-scatter.8.cloned.1.call-done = f32[64,512]{1,0:T(8,128)} async-done(((f32[1024,512]{1,0:T(8,128)}), f32[64,512]{1,0:T(8,128)}) %reduce-scatter.8.cloned.1.call-update) | async-done | bytes 131088 | tf_op jit(solution)/shard_map/reduce_scatter | solution.py:297
  (377 shorter events, 510.0 us)
Async XLA Ops:
  7.2 74.3 %copy-start = (bf16[1,1024,1024]{2,1,0:T(8,128)(2,1)S(1)}, bf16[1,1024,1024]{2,1,0:T(8,128)(2,1)}, u32[]{:S(2)}) copy-start(bf16[1,1024,1024]{2,1,0:T(8,128)(2,1)} %param.15) | copy-start | bytes 6291460
  7.2 74.3 %all-gather.5.cloned.1.call-start = ((), (), s32[]{:S(2)}) async-start(), calls=%async_computation.7 | async-start | bytes 3342336 | tf_op jit(solution)/shard_map/all_gather | solution.py:83
  7.9 169.2 %all-gather.7.cloned.1.call-start = ((), (), s32[]{:S(2)}) async-start(), calls=%async_computation.8 | async-start | bytes 10485760 | tf_op jit(solution)/shard_map/all_gather | solution.py:104
  55.5 32.1 %copy-start.26 = (f32[1024]{0:T(1024)}, f32[1024]{0:T(1024)S(1)}, u32[]{:S(2)}) copy-start(f32[1024]{0:T(1024)S(1)} %convert_element_type.129) | copy-start | bytes 12292
  57.5 30.2 %copy-start.22 = (f32[1024]{0:T(1024)}, f32[1024]{0:T(1024)S(1)}, u32[]{:S(2)}) copy-start(f32[1024]{0:T(1024)S(1)} %broadcast_multiply_fusion.5) | copy-start | bytes 12292
  59.8 27.9 %copy-start.28 = (f32[1024]{0:T(1024)}, f32[1024]{0:T(1024)S(1)}, u32[]{:S(2)}) copy-start(f32[1024]{0:T(1024)S(1)} %add_rsqrt_fusion.1) | copy-start | bytes 12292
  90.8 222.9 %all-gather.9.cloned.1.call-start = ((), (), s32[]{:S(2)}) async-start(), calls=%async_computation.9 | async-start | bytes 1114112 | tf_op jit(solution)/shard_map/all_gather | solution.py:84
  91.6 247.8 %all-reduce.15.cloned.1.call-start = ((), (), s32[]{:S(2)}) async-start(), calls=%async_computation.10 | async-start | bytes 4194304 | tf_op jit(solution)/shard_map/psum | solution.py:135
  313.8 4.9 copy-start.18
  352.9 10.3 copy-start.32
  356.4 99.6 %all-to-all-start = ((bf16[16,80,1024]{2,1,0:T(8,128)(2,1)}), bf16[16,80,1024]{2,1,0:T(8,128)(2,1)}, u32[]{:S(2)}, u32[]{:S(2)}) async-start(bf16[16,80,1024]{2,1,0:T(8,128)(2,1)} %bitcast.365), calls=%async_computation | async-start | bytes 5242880 | tf_op jit(solution)/shard_map/all_to_all | solution.py:157
  444.3 264.7 %copy-start.16 = (f32[1024,16]{0,1:T(8,128)}, f32[1024,16]{0,1:T(8,128)S(1)}, u32[]{:S(2)}) copy-start(f32[1024,16]{0,1:T(8,128)S(1)} %get-tuple-element.481) | copy-start | bytes 196612
  444.3 264.7 %copy-start.20 = (f32[1024]{0:T(1024)}, f32[1024]{0:T(1024)S(1)}, u32[]{:S(2)}) copy-start(f32[1024]{0:T(1024)S(1)} %get-tuple-element.480) | copy-start | bytes 12292
  444.3 264.6 %copy-start.24 = (f32[1024]{0:T(1024)}, f32[1024]{0:T(1024)S(1)}, u32[]{:S(2)}) copy-start(f32[1024]{0:T(1024)S(1)} %fusion.112) | copy-start | bytes 12292
  455.9 57.2 %all-to-all-start.2 = ((bf16[16,80,1024]{2,1,0:T(8,128)(2,1)}), bf16[16,80,1024]{2,1,0:T(8,128)(2,1)}, u32[]{:S(2)}, u32[]{:S(2)}) async-start(bf16[16,80,1024]{2,1,0:T(8,128)(2,1)} %bitcast.367), calls=%async_computation.2 | async-start | bytes 5242880 | tf_op jit(solution)/shard_map/all_to_all | solution.py:193
  466.3 104.9 %all-reduce.21.cloned.1.call-start = ((), (), s32[]{:S(2)}) async-start(), calls=%async_computation.16 | async-start | bytes 10485760 | tf_op jit(solution)/shard_map/psum | solution.py:163
  466.4 12.6 copy-start.34
  475.0 4.0 copy-start.38
  513.1 15.5 copy-start.35
  528.6 7.5 copy-start.37
  638.6 55.6 %all-to-all-start.1 = ((bf16[16,80,1024]{2,1,0:T(8,128)(2,1)}), bf16[16,80,1024]{2,1,0:T(8,128)(2,1)}, u32[]{:S(2)}, u32[]{:S(2)}) async-start(bf16[16,80,1024]{2,1,0:T(8,128)(2,1)} %get-tuple-element.464), calls=%async_computation.1 | async-start | bytes 5242880 | tf_op jit(solution)/shard_map/all_to_all | solution.py:164
  643.0 458.0 %reduce-scatter.6.cloned.1.call-start = ((), (), s32[]{:S(2)}) async-start(), calls=%async_computation.11 | async-start | bytes 10485760 | tf_op jit(solution)/shard_map/reduce_scatter | solution.py:280
  1008.2 172.6 %reduce-scatter.10.cloned.1.call-start = ((), (), s32[]{:S(2)}) async-start(), calls=%async_computation.14 | async-start | bytes 557056
  1011.5 93.5 %copy-start.15 = (bf16[1024,1,512]{2,0,1:T(8,128)(2,1)S(1)}, bf16[1024,1,512]{2,0,1:T(8,128)(2,1)}, u32[]{:S(2)}) copy-start(bf16[1024,1,512]{2,0,1:T(8,128)(2,1)} %copy.50) | copy-start | bytes 3145732
  1015.0 185.8 %all-reduce.17.cloned.1.call-start = ((), (), s32[]{:S(2)}) async-start(), calls=%async_computation.12 | async-start | bytes 4194304 | tf_op jit(solution)/shard_map/psum | solution.py:292
  1105.0 7.5 copy-start.1
  1105.0 7.5 copy-start.23
  1105.0 7.5 copy-start.27
  1105.0 7.5 copy-start.29
  1112.4 352.4 %all-reduce.19.cloned.1.call-start = ((), (), s32[]{:S(2)}) async-start(), calls=%async_computation.15 | async-start | bytes 16777216
  1130.0 418.1 %reduce-scatter.8.cloned.1.call-start = ((), (), s32[]{:S(2)}) async-start(), calls=%async_computation.13 | async-start | bytes 2228224 | tf_op jit(solution)/shard_map/reduce_scatter | solution.py:297
  1159.4 44.9 %copy-start.33 = (f32[1024]{0:T(1024)S(1)}, f32[1024]{0:T(1024)}, u32[]{:S(2)}) copy-start(f32[1024]{0:T(1024)} %get-tuple-element.418) | copy-start | bytes 12292
  (34 other events, 85.8 us)
Sparse Core Ops, SparseCore 0:
  10.8 70.7 all-gather.4
  91.0 86.0 all-gather.6
  179.9 55.1 all-gather.8
  318.1 21.2 all-reduce.14
  536.2 34.9 all-reduce.20
  1008.3 92.6 reduce-scatter.5
  1103.3 77.4 reduce-scatter.9
  1183.1 17.6 all-reduce.16
  1206.8 257.9 all-reduce.18
  1467.5 80.5 reduce-scatter.7
where the time goes:
time: 1560 us
  waiting for transfers between devices  641 us (41%)
  matrix products  436 us (28%)
  blocking collectives  235 us (15%)
  local copies, waits for them, and re-layouts  103 us (7%)
  other arithmetic  100 us (6%)
  starting transfers between devices  22.6 us (1%)
  between operations  17.1 us (1%)
    unnamed x12, waiting for transfers between devices  232 us
    unnamed x2, blocking collectives  88.6 us
    dot_general x16, matrix products, score_block(): jnp.einsum('sqhd,skhd->sqhk', query, keys, preferred_element_type=jnp.flo...  87 us
    reduce_scatter x1, waiting for transfers between devices, local(): lax.psum_scatter(grad_all_pairs.astype(jnp.bfloat16), 'ctx', scatter_dime...  86 us
    all_gather x1, waiting for transfers between devices, local(): piece = lax.all_gather(pairs, 'ctx', axis=1, tiled=True)  83.6 us
    reduce_scatter x1, waiting for transfers between devices, local(): lax.psum_scatter(grad_proj, ('shard', 'ctx'), scatter_dimension=0, tiled=...  81.3 us
    all_gather x1, blocking collectives, local(): lax.all_gather(router, ('shard', 'ctx'), axis=0, tiled=True)  78.6 us
    dot_general x8, matrix products, inner(): jnp.einsum('sqhd,skhd->sqhk', grad_mixed, values, preferred_element_type=...  75.8 us
  transfers between devices with their start and end apart: 13, of which 11 were waited for; matrix products, arithmetic and copies ran while one was open for 17% of the time, Pallas kernels for 0%

commit v1 on v0

v1 whole, which is shorter than its diff:
```python
import functools

import jax
import jax.numpy as jnp
from jax import lax
from jax.experimental import pallas as pl
from jax.experimental.pallas import tpu as pltpu
from jax.sharding import PartitionSpec as P

HEAD_DIM = 64
EPSILON = 1e-05
MASKED = -1e30
LOG2E = 1.4426950408889634
BLOCK = 512
MESH = pl.DeviceIdType.MESH
BF16 = jnp.bfloat16
F32 = jnp.float32


class Item:
    def __init__(self, group, ins, outs, src, dst, relay=None, block=None, keep=True):
        self.group, self.ins, self.outs = group, ins, outs
        self.src, self.dst, self.relay, self.block, self.keep = src, dst, relay, block, keep


def exchange(name, collective_id, sizes, items):
    shards, ctxs, tps = sizes
    count_all = shards * ctxs
    operands = [item.ins for item in items]
    out_shapes = [shape for item in items for shape in item.outs]
    scratch = []
    for item in items:
        n = {"ctx": ctxs, "all": count_all, "pair": 1}[item.group]
        item.n = n
        scratch += [pltpu.SemaphoreType.DMA((n,)) for _ in range(4)]
        scratch.append(pltpu.SemaphoreType.DMA((2,)))
        if item.keep:
            scratch.append(pltpu.VMEM(item.block, item.ins.dtype))
    wide = any(item.group == "all" for item in items)
    near = any(item.group == "ctx" for item in items)
    paired = any(item.group == "pair" or item.relay is not None for item in items)

    def body(*refs):
        in_refs = refs[: len(operands)]
        out_refs = refs[len(operands) : len(operands) + len(out_shapes)]
        rest = list(refs[len(operands) + len(out_shapes) :])
        me_s, me_c, me_t = lax.axis_index("shard"), lax.axis_index("ctx"), lax.axis_index("tp")
        me_all = me_s * ctxs + me_c
        other = tps - 1 - me_t
        partner = {"tp": other}

        def place(group, p):
            if group == "ctx":
                return {"ctx": p}
            return {"shard": p // ctxs, "ctx": p % ctxs}

        barrier = pltpu.get_barrier_semaphore()
        group, size, me = ("all", count_all, me_all) if wide else ("ctx", ctxs, me_c)
        greeted = 0
        if wide or near:

            def greet(k, carry):
                peer = lax.rem(me + k, size)
                pl.semaphore_signal(
                    barrier, inc=1, device_id=place(group, peer), device_id_type=MESH
                )
                return carry

            lax.fori_loop(1, size, greet, 0)
            greeted += size - 1
        if paired:
            pl.semaphore_signal(barrier, inc=1, device_id=partner, device_id_type=MESH)
            greeted += 1
        pl.semaphore_wait(barrier, greeted)

        jobs = []
        at = 0
        for item, source in zip(items, in_refs):
            outs = out_refs[at : at + len(item.outs)]
            at += len(item.outs)
            sems = [rest.pop(0) for _ in range(5)]
            stage = rest.pop(0) if item.keep else None
            jobs.append((item, source, outs, sems, stage))

        def make(item, source, outs, sems, k, peer, sender):
            mine = {"ctx": me_c, "all": me_all}[item.group]
            return pltpu.make_async_remote_copy(
                src_ref=item.src(source, peer),
                dst_ref=item.dst(outs[0], sender, me_t),
                send_sem=sems[0].at[k],
                recv_sem=sems[1].at[sender],
                device_id=place(item.group, peer),
                device_id_type=MESH,
            )

        def make_relay(item, source, outs, sems, k, member, first):
            mine = {"ctx": me_c, "all": me_all, "pair": 0}[item.group]
            return pltpu.make_async_remote_copy(
                src_ref=item.src(source, mine) if first else item.dst(outs[0], member, me_t),
                dst_ref=item.relay(outs[-1], member, me_t),
                send_sem=sems[2].at[k],
                recv_sem=sems[3].at[member],
                device_id=partner,
                device_id_type=MESH,
            )

        def each(n, act):
            def step(k, carry):
                act(k)
                return carry

            lax.fori_loop(1, n, step, 0)

        mine_of = {"ctx": me_c, "all": me_all, "pair": 0}
        for item, source, outs, sems, stage in jobs:
            mine = mine_of[item.group]
            if item.n > 1:

                def send(k, item=item, source=source, outs=outs, sems=sems, mine=mine):
                    peer = lax.rem(mine + k, item.n)
                    make(item, source, outs, sems, k, peer, mine).start()

                each(item.n, send)
            if item.relay is not None:
                make_relay(item, source, outs, sems, 0, mine, True).start()
        for item, source, outs, sems, stage in jobs:
            if item.keep:
                pltpu.make_async_copy(
                    item.src(source, mine_of[item.group]), stage, sems[4].at[0]
                ).start()
        for item, source, outs, sems, stage in jobs:
            if item.keep:
                mine = mine_of[item.group]
                pltpu.make_async_copy(item.src(source, mine), stage, sems[4].at[0]).wait()
                pltpu.make_async_copy(
                    stage, item.dst(outs[0], mine, me_t), sems[4].at[1]
                ).start()
        for item, source, outs, sems, stage in jobs:
            mine = mine_of[item.group]
            if item.n > 1:

                def take(k, item=item, source=source, outs=outs, sems=sems, mine=mine):
                    member = lax.rem(mine + item.n - k, item.n)
                    peer = lax.rem(mine + k, item.n)
                    make(item, source, outs, sems, k, peer, member).wait_recv()
                    if item.relay is not None:
                        make_relay(item, source, outs, sems, k, member, False).start()

                each(item.n, take)
        for item, source, outs, sems, stage in jobs:
            mine = mine_of[item.group]
            if item.n > 1:

                def sent(k, item=item, source=source, outs=outs, sems=sems, mine=mine):
                    peer = lax.rem(mine + k, item.n)
                    make(item, source, outs, sems, k, peer, mine).wait_send()

                each(item.n, sent)
            if item.relay is not None:
                make_relay(item, source, outs, sems, 0, mine, True).wait()
                if item.n > 1:

                    def passed(k, item=item, source=source, outs=outs, sems=sems, mine=mine):
                        member = lax.rem(mine + item.n - k, item.n)
                        make_relay(item, source, outs, sems, k, member, False).wait()

                    each(item.n, passed)
            if item.keep:
                pltpu.make_async_copy(
                    stage, item.dst(outs[0], mine, me_t), sems[4].at[1]
                ).wait()

    anywhere = pl.BlockSpec(memory_space=pl.ANY)
    return pl.pallas_call(
        body,
        name=name,
        out_shape=tuple(out_shapes),
        in_specs=[anywhere] * len(operands),
        out_specs=tuple([anywhere] * len(out_shapes)),
        scratch_shapes=scratch,
        compiler_params=pltpu.CompilerParams(collective_id=collective_id, has_side_effects=True),
    )(*operands)


def nt(left, right):
    return lax.dot_general(left, right, (((1,), (1,)), ((), ())), preferred_element_type=F32)


def nn(left, right):
    return lax.dot_general(left, right, (((1,), (0,)), ((), ())), preferred_element_type=F32)


def tn(left, right):
    return lax.dot_general(left, right, (((0,), (0,)), ((), ())), preferred_element_type=F32)


def stacked(rows, heads):
    lane = lax.broadcasted_iota(jnp.int32, rows.shape, 1) // HEAD_DIM
    return jnp.concatenate([jnp.where(lane == h, rows, jnp.zeros_like(rows)) for h in range(heads)], 0)


def merged(pieces, heads):
    block = pieces.shape[0] // heads
    lane = lax.broadcasted_iota(jnp.int32, (block, pieces.shape[1]), 1) // HEAD_DIM
    total = pieces[:block]
    for h in range(1, heads):
        total = jnp.where(lane == h, pieces[h * block : (h + 1) * block], total)
    return total


def forward_kernel(heads, size, len_ref, q_ref, k_ref, v_ref, o_ref, lse_ref):
    i = pl.program_id(0)
    length = len_ref[0]
    scale = HEAD_DIM ** (-0.5)
    queries = stacked((q_ref[...].astype(F32) * scale).astype(BF16), heads)
    tall = heads * size
    row = lax.broadcasted_iota(jnp.int32, (tall, 1), 0) % size
    limit = jnp.minimum(i * size + row, length - 1)
    full = (jnp.minimum(i * size, length - 1) + 1) // size
    every = (jnp.minimum((i + 1) * size, length) + size - 1) // size

    def step(masked, j, state):
        top, total, accum = state
        place = pl.ds(pl.multiple_of(j * size, size), size)
        scores = nt(queries, k_ref[place, :]) * LOG2E
        if masked:
            column = j * size + lax.broadcasted_iota(jnp.int32, (tall, size), 1)
            scores = jnp.where(column <= limit, scores, MASKED)
        new_top = jnp.maximum(top, jnp.max(scores, axis=-1, keepdims=True))
        factor = jnp.exp2(top - new_top)
        weights = jnp.exp2(scores - new_top)
        total = total * factor + jnp.sum(weights, axis=-1, keepdims=True)
        accum = accum * factor + nn(weights.astype(BF16), v_ref[place, :])
        return new_top, total, accum

    state = (
        jnp.full((tall, 1), MASKED, F32),
        jnp.zeros((tall, 1), F32),
        jnp.zeros((tall, heads * HEAD_DIM), F32),
    )
    state = lax.fori_loop(0, full, functools.partial(step, False), state)
    top, total, accum = lax.fori_loop(full, every, functools.partial(step, True), state)
    o_ref[...] = merged(accum / total, heads).astype(BF16)
    log_total = jnp.broadcast_to(top + jnp.log2(total), (tall, 128))
    lse_ref[0] = jnp.transpose(log_total)[:1, :]


def attention_forward(projected, lengths, heads):
    count, _ = projected.shape
    wide = heads * HEAD_DIM
    size = BLOCK
    blocks = count // size
    return pl.pallas_call(
        functools.partial(forward_kernel, heads, size),
        name="attention_forward",
        out_shape=(
            jax.ShapeDtypeStruct((count, wide), BF16),
            jax.ShapeDtypeStruct((blocks, 1, heads * size), F32),
        ),
        grid_spec=pltpu.PrefetchScalarGridSpec(
            num_scalar_prefetch=1,
            grid=(blocks,),
            in_specs=[
                pl.BlockSpec((size, wide), lambda i, n: (i, 0)),
                pl.BlockSpec((count, wide), lambda i, n: (0, 1)),
                pl.BlockSpec((count, wide), lambda i, n: (0, 2)),
            ],
            out_specs=[
                pl.BlockSpec((size, wide), lambda i, n: (i, 0)),
                pl.BlockSpec((1, 1, heads * size), lambda i, n: (i, 0, 0)),
            ],
        ),
        cost_estimate=pl.CostEstimate(
            flops=16 * count * count * wide,
            bytes_accessed=8 * count * wide,
            transcendentals=heads * count * count // 2,
        ),
    )(lengths, projected, projected, projected)


def backward_kernel(
    heads, size, blocks, len_ref, q_ref, k_ref, v_ref, o_ref, do_ref, lse_ref, out_ref,
    queries, grads, delta, grad_queries,
):
    j = pl.program_id(0)
    length = len_ref[0]
    scale = HEAD_DIM ** (-0.5)
    tall = heads * size
    wide = heads * HEAD_DIM

    @pl.when(j == 0)
    def _():
        def prepare(i, carry):
            place = pl.ds(pl.multiple_of(i * size, size), size)
            tall_place = pl.ds(pl.multiple_of(i * tall, tall), tall)
            queries[tall_place, :] = stacked((q_ref[place, :].astype(F32) * scale).astype(BF16), heads)
            grad = do_ref[place, :]
            grads[tall_place, :] = stacked(grad, heads)
            product = jnp.transpose(grad.astype(F32) * o_ref[place, :].astype(F32))
            delta[i] = jnp.concatenate(
                [
                    jnp.sum(product[h * HEAD_DIM : (h + 1) * HEAD_DIM], axis=0, keepdims=True)
                    for h in range(heads)
                ],
                axis=1,
            )
            grad_queries[i] = jnp.zeros((wide, tall), F32)
            return carry

        lax.fori_loop(0, blocks, prepare, 0)

    keys = k_ref[...]
    values = v_ref[...]
    keys_turned = jnp.transpose(keys.astype(F32)).astype(BF16)
    column = j * size + lax.broadcasted_iota(jnp.int32, (size, tall), 0)
    inner = lax.broadcasted_iota(jnp.int32, (1, tall), 1) % size

    def step(masked, i, state):
        grad_keys, grad_values = state
        tall_place = pl.ds(pl.multiple_of(i * tall, tall), tall)
        query = queries[tall_place, :]
        grad = grads[tall_place, :]
        power = nt(keys, query) * LOG2E - lse_ref[i]
        if masked:
            limit = jnp.minimum(i * size + inner, length - 1)
            power = jnp.where(column <= limit, power, MASKED)
        weights = jnp.exp2(power)
        grad_values = grad_values + nn(weights.astype(BF16), grad)
        grad_scores = (weights * (nt(values, grad) - delta[i])).astype(BF16)
        grad_keys = grad_keys + nn(grad_scores, query)
        grad_queries[i] += nn(keys_turned, grad_scores)
        return grad_keys, grad_values

    state = (jnp.zeros((size, wide), F32), jnp.zeros((size, wide), F32))
    crosses = (j + 1) * size > length
    begin = jnp.where(j * size < length, j, blocks)
    middle = jnp.where(crosses, blocks, j + 1)
    state = lax.fori_loop(begin, middle, functools.partial(step, True), state)
    grad_keys, grad_values = lax.fori_loop(middle, blocks, functools.partial(step, False), state)
    place = pl.ds(pl.multiple_of(j * size, size), size)
    out_ref[place, wide : 2 * wide] = grad_keys.astype(BF16)
    out_ref[place, 2 * wide : 3 * wide] = grad_values.astype(BF16)

    @pl.when(j == blocks - 1)
    def _():
        def finish(i, carry):
            block_place = pl.ds(pl.multiple_of(i * size, size), size)
            turned = jnp.transpose(grad_queries[i])
            out_ref[block_place, :wide] = (merged(turned, heads) * scale).astype(BF16)
            return carry

        lax.fori_loop(0, blocks, finish, 0)


def attention_backward(projected, mixed, grad_mixed, lse, lengths, heads):
    count, _ = projected.shape
    wide = heads * HEAD_DIM
    size = BLOCK
    blocks = count // size
    tall = heads * size
    return pl.pallas_call(
        functools.partial(backward_kernel, heads, size, blocks),
        name="attention_backward",
        out_shape=jax.ShapeDtypeStruct((count, 3 * wide), BF16),
        grid_spec=pltpu.PrefetchScalarGridSpec(
            num_scalar_prefetch=1,
            grid=(blocks,),
            in_specs=[
                pl.BlockSpec((count, wide), lambda j, n: (0, 0)),
                pl.BlockSpec((size, wide), lambda j, n: (j, 1)),
                pl.BlockSpec((size, wide), lambda j, n: (j, 2)),
                pl.BlockSpec((count, wide), lambda j, n: (0, 0)),
                pl.BlockSpec((count, wide), lambda j, n: (0, 0)),
                pl.BlockSpec((blocks, 1, tall), lambda j, n: (0, 0, 0)),
            ],
            out_specs=pl.BlockSpec((count, 3 * wide), lambda j, n: (0, 0)),
            scratch_shapes=[
                pltpu.VMEM((heads * count, wide), BF16),
                pltpu.VMEM((heads * count, wide), BF16),
                pltpu.VMEM((blocks, 1, tall), F32),
                pltpu.VMEM((blocks, wide, tall), F32),
            ],
        ),
        cost_estimate=pl.CostEstimate(
            flops=40 * count * count * wide,
            bytes_accessed=16 * count * wide,
            transcendentals=heads * count * count // 2,
        ),
    )(lengths, projected, projected, projected, mixed, grad_mixed, lse)


def normed(values):
    center = values - jnp.mean(values, axis=-1, keepdims=True)
    inverse = lax.rsqrt(jnp.mean(center * center, axis=-1, keepdims=True) + EPSILON)
    return center * inverse, inverse


def norm_back(scaled, unit, inverse):
    return inverse * (
        scaled
        - jnp.mean(scaled, axis=-1, keepdims=True)
        - unit * jnp.mean(scaled * unit, axis=-1, keepdims=True)
    )


def shape_of(extent, dtype):
    return jax.ShapeDtypeStruct(extent, dtype)


def local(
    sizes, tokens, lengths, routes, weight_qkv, weight_proj, router, gain_one, gain_two,
    w_in, w_out, cotangent,
):
    shards, ctxs, tps = sizes
    group = ("shard", "ctx")
    groups = shards * ctxs
    slots, count, width = tokens.shape
    assert slots == 1 and tps == 2
    head_width = weight_qkv.shape[2]
    wide = head_width // ctxs
    heads = wide // HEAD_DIM
    rows = weight_qkv.shape[1]
    experts = router.shape[1]
    capacity = max(2, (5 * count + 4 * experts - 1) // (4 * experts))
    assert capacity % 2 == 0
    half_cap = capacity // 2
    half = count // tps
    length_all = ctxs * count
    ctx_rank = lax.axis_index("ctx")
    tp_rank = lax.axis_index("tp")

    inputs = tokens[0].astype(F32)
    own_half = lax.dynamic_slice_in_dim(tokens[0], tp_rank * half, half, 0).astype(F32)
    unit_half = normed(own_half)[0].astype(BF16)
    scaled_qkv = (weight_qkv.astype(F32) * gain_one.astype(F32)[None, :, None]).astype(BF16)
    by_ctx = scaled_qkv.reshape(3, rows, ctxs, wide).transpose(2, 1, 0, 3).reshape(ctxs, rows, 3 * wide)
    pad = -(-(experts + 1) // 128) * 128
    small = jnp.concatenate(
        [router, gain_two[:, None], jnp.zeros((rows, pad - experts - 1), BF16)], axis=1
    )
    sent_weights = jnp.concatenate(
        [by_ctx, jnp.broadcast_to(small[None], (ctxs, rows, pad))], axis=2
    )
    whole_qkv = lax.all_gather(
        by_ctx.transpose(1, 0, 2).reshape(rows, ctxs * 3 * wide), group, axis=0, tiled=True
    )
    whole_proj = lax.all_gather(weight_proj, group, axis=0, tiled=True)

    unit_all, got_weights = exchange(
        "gather_rows", 1, sizes,
        [
            Item(
                "ctx", unit_half, [shape_of((ctxs, tps, half, width), BF16)],
                lambda ref, p: ref,
                lambda ref, q, t: ref.at[q, t],
                relay=lambda ref, q, t: ref.at[q, t],
                block=(half, width),
            ),
            Item(
                "all", sent_weights, [shape_of((groups, rows, 3 * wide + pad), BF16)],
                lambda ref, p: ref.at[p % ctxs],
                lambda ref, q, t: ref.at[q],
                block=(rows, 3 * wide + pad),
            ),
        ],
    )
    unit_all = unit_all.reshape(length_all, width)
    got_weights = got_weights.reshape(width, 3 * wide + pad)
    own_qkv = got_weights[:, : 3 * wide]
    full_router = got_weights[:, 3 * wide : 3 * wide + experts]
    full_two = got_weights[:, 3 * wide + experts].astype(F32)

    places = ctx_rank * count + jnp.arange(count, dtype=jnp.int32)
    route = routes.reshape(count)
    valid = places < lengths[0]
    route_hot = route[:, None] == jnp.arange(experts, dtype=jnp.int32)[None, :]
    counted = (route_hot & valid[:, None]).astype(BF16)
    order = jnp.arange(count, dtype=jnp.int32)
    below = (order[:, None] > order[None, :]).astype(BF16)
    earlier = nn(below, counted)
    place = jnp.sum(earlier * counted.astype(F32), axis=1).astype(jnp.int32)
    kept = valid & (place < capacity)
    target = jnp.where(kept, route * capacity + place, experts * capacity)
    slot = jnp.arange(experts * half_cap, dtype=jnp.int32)
    slot = (slot // half_cap) * capacity + slot % half_cap
    own_slot = slot + tp_rank * half_cap
    par_slot = slot + (1 - tp_rank) * half_cap
    pick_own = (own_slot[:, None] == target[None, :]).astype(BF16)
    pick_par = (par_slot[:, None] == target[None, :]).astype(BF16)

    cot = cotangent[0]
    sent_cot = nn(pick_own, cot).astype(BF16).reshape(experts, half_cap, width)
    got_cot = lax.all_to_all(sent_cot, group, split_axis=0, concat_axis=0, tiled=True)

    projected = nn(unit_all, own_qkv).astype(BF16)
    mixed_heads, lse = attention_forward(projected, lengths, heads)

    mixed_own, mixed_par, proj_par, qkv_par, cot_par = exchange(
        "mixed_home", 2, sizes,
        [
            Item(
                "ctx", mixed_heads,
                [shape_of((count, head_width), BF16), shape_of((count, head_width), BF16)],
                lambda ref, p: ref.at[pl.ds(pl.multiple_of(p * count, count), count), :],
                lambda ref, q, t: ref.at[:, pl.ds(pl.multiple_of(q * wide, wide), wide)],
                relay=lambda ref, q, t: ref.at[:, pl.ds(pl.multiple_of(q * wide, wide), wide)],
                block=(count, wide),
            ),
            Item(
                "pair", whole_proj, [shape_of(whole_proj.shape, BF16)],
                lambda ref, p: ref, None, relay=lambda ref, q, t: ref, keep=False,
            ),
            Item(
                "pair", whole_qkv, [shape_of(whole_qkv.shape, BF16)],
                lambda ref, p: ref, None, relay=lambda ref, q, t: ref, keep=False,
            ),
            Item(
                "pair", got_cot, [shape_of(got_cot.shape, BF16)],
                lambda ref, p: ref, None, relay=lambda ref, q, t: ref, keep=False,
            ),
        ],
    )

    middle = inputs + nt(mixed_own, whole_proj) + nt(mixed_par, proj_par)
    unit_two, inverse_two = normed(middle)
    second = (unit_two * full_two).astype(BF16)
    probs = jax.nn.softmax(nn(second, full_router), axis=-1)
    gate = jnp.sum(jnp.where(route_hot, probs, 0.0), axis=1)
    sent_rows = nn(pick_own, second).astype(BF16).reshape(experts, half_cap, width)
    gate_rows = jnp.sum(
        jnp.where(own_slot[:, None] == target[None, :], gate[None, :], 0.0), axis=1
    ).reshape(experts, half_cap)
    lanes = -(-half_cap // 128) * 128
    gate_rows = jnp.broadcast_to(
        jnp.pad(gate_rows, ((0, 0), (0, lanes - half_cap)))[:, None, :], (experts, 8, lanes)
    )

    got_rows, got_gates = exchange(
        "dispatch", 3, sizes,
        [
            Item(
                "all", sent_rows, [shape_of((tps, groups, half_cap, width), BF16)],
                lambda ref, p: ref.at[p],
                lambda ref, q, t: ref.at[0, q],
                relay=lambda ref, q, t: ref.at[1, q],
                block=(half_cap, width),
            ),
            Item(
                "all", gate_rows, [shape_of((tps, groups, 8, lanes), F32)],
                lambda ref, p: ref.at[p],
                lambda ref, q, t: ref.at[0, q],
                relay=lambda ref, q, t: ref.at[1, q],
                block=(8, lanes),
            ),
        ],
    )

    total_rows = tps * groups * half_cap
    arrived = got_rows.reshape(total_rows, width)
    gates = got_gates[:, :, 0, :half_cap].reshape(total_rows)
    cot_rows = jnp.concatenate([got_cot, cot_par], axis=0).reshape(total_rows, width)
    grad_rows = (gates[:, None] * cot_rows.astype(F32)).astype(BF16)
    pre = nn(arrived, w_in[0])
    hidden, gelu_back = jax.vjp(jax.nn.gelu, pre)
    hidden = hidden.astype(BF16)
    partial_out = nn(hidden, w_out[0]).astype(BF16).reshape(tps, groups, half_cap, width)

    def pair_item(array, index):
        return Item(
            "pair", array, [shape_of(array.shape[1:], BF16)],
            lambda ref, p: ref.at[index], None, relay=lambda ref, q, t: ref, keep=False,
        )

    (out_par,) = exchange("sum_out", 4, sizes, [pair_item(partial_out, 1)])
    summed = (partial_out[0].astype(F32) + out_par.astype(F32)).astype(BF16)
    going_back = lax.all_to_all(summed, group, split_axis=0, concat_axis=0, tiled=True)

    grad_w_out = tn(hidden, grad_rows)[None]
    grad_hidden = nt(grad_rows, w_out[0])
    grad_pre = gelu_back(grad_hidden)[0].astype(BF16)
    partial_grad = nt(grad_pre, w_in[0]).astype(BF16).reshape(tps, groups, half_cap, width)
    grad_w_in = tn(arrived, grad_pre)[None]

    (grad_par,) = exchange("sum_grad", 5, sizes, [pair_item(partial_grad, 1)])
    grad_summed = (partial_grad[0].astype(F32) + grad_par.astype(F32)).astype(BF16)
    grad_home, back_par = exchange(
        "grad_home", 6, sizes,
        [
            Item(
                "all", grad_summed, [shape_of((tps, groups, half_cap, width), BF16)],
                lambda ref, p: ref.at[p],
                lambda ref, q, t: ref.at[0, q],
                relay=lambda ref, q, t: ref.at[1, q],
                block=(half_cap, width),
            ),
            Item(
                "pair", going_back, [shape_of(going_back.shape, BF16)],
                lambda ref, p: ref, None, relay=lambda ref, q, t: ref, keep=False,
            ),
        ],
    )

    slots_half = experts * half_cap
    fetched = tn(pick_own, going_back.reshape(slots_half, width)) + tn(
        pick_par, back_par.reshape(slots_half, width)
    )
    grad_home = grad_home.reshape(tps, slots_half, width)
    grad_home_rows = tn(pick_own, grad_home[0]) + tn(pick_par, grad_home[1])
    kept_value = kept.astype(F32)
    valid_value = valid.astype(F32)
    output = (
        (valid_value[:, None] * (middle + (kept_value * gate)[:, None] * fetched))
        .astype(BF16)
        .reshape(slots, count, width)
    )
    grad_out = valid_value[:, None] * cot.astype(F32)
    grad_gate = kept_value * jnp.sum(grad_out * fetched, axis=1)
    grad_logits = ((grad_gate * gate)[:, None] * (route_hot.astype(F32) - probs)).astype(BF16)
    grad_second = grad_home_rows + nt(grad_logits, full_router)
    grad_middle = grad_out + norm_back(grad_second * full_two, unit_two, inverse_two)
    grad_branch = grad_middle.astype(BF16)
    grad_mixed_own = nn(grad_branch, whole_proj).astype(BF16)

    (grad_mixed,) = exchange(
        "grad_mixed", 7, sizes,
        [
            Item(
                "ctx", grad_mixed_own, [shape_of((length_all, wide), BF16)],
                lambda ref, p: ref.at[:, pl.ds(pl.multiple_of(p * wide, wide), wide)],
                lambda ref, q, t: ref.at[pl.ds(pl.multiple_of(q * count, count), count), :],
                block=(count, wide),
            ),
        ],
    )
    grad_router = tn(second, grad_logits)
    grad_gain_two = jnp.sum(grad_second * unit_two, axis=0)
    grad_proj = tn(grad_branch, mixed_own)
    packed = jnp.concatenate(
        [grad_proj, grad_router, grad_gain_two[:, None], jnp.zeros((width, pad - experts - 1), F32)],
        axis=1,
    )
    owned = lax.psum_scatter(packed, group, scatter_dimension=0, tiled=True)
    owned_proj = owned[:, :head_width]
    owned_router = owned[:, head_width : head_width + experts]
    owned_two = owned[:, head_width + experts]

    grad_projected = attention_backward(projected, mixed_heads, grad_mixed, lse, lengths, heads)
    grad_weight = tn(unit_all, grad_projected).astype(BF16).reshape(groups, rows, 3 * wide)
    grad_own, grad_par, got_grad = exchange(
        "grad_projected", 8, sizes,
        [
            Item(
                "ctx", grad_projected,
                [shape_of((count, 3 * head_width), BF16), shape_of((count, 3 * head_width), BF16)],
                lambda ref, p: ref.at[pl.ds(pl.multiple_of(p * count, count), count), :],
                lambda ref, q, t: ref.at[:, pl.ds(pl.multiple_of(q * 3 * wide, wide), 3 * wide)],
                relay=lambda ref, q, t: ref.at[:, pl.ds(pl.multiple_of(q * 3 * wide, wide), 3 * wide)],
                block=(count, 3 * wide),
            ),
            Item(
                "all", grad_weight, [shape_of((groups, rows, 3 * wide), BF16)],
                lambda ref, p: ref.at[p],
                lambda ref, q, t: ref.at[q],
                block=(rows, 3 * wide),
            ),
        ],
    )
    scaled_first = nt(grad_own, whole_qkv) + nt(grad_par, qkv_par)
    unit_one, inverse_one = normed(inputs)
    grad_tokens = (grad_middle + norm_back(scaled_first, unit_one, inverse_one)).reshape(
        slots, count, width
    )
    raw = (
        jnp.sum(got_grad.astype(F32).reshape(shards, ctxs, rows, 3, wide), axis=0)
        .transpose(2, 1, 0, 3)
        .reshape(3, rows, head_width)
    )
    owned_qkv = raw * gain_one.astype(F32)[None, :, None]
    owned_one = lax.psum(jnp.sum(raw * weight_qkv.astype(F32), axis=(0, 2)), "tp")
    return (
        output,
        grad_tokens,
        owned_qkv,
        owned_proj,
        owned_router,
        owned_one,
        owned_two,
        grad_w_in,
        grad_w_out,
    )


def solution(mesh):
    sizes = (mesh.shape["shard"], mesh.shape["ctx"], mesh.shape["tp"])
    return jax.shard_map(
        functools.partial(local, sizes),
        mesh=mesh,
        in_specs=(
            P("shard", "ctx", None),
            P("shard"),
            P("shard", "ctx", None),
            P(None, ("shard", "ctx"), "tp"),
            P(("shard", "ctx"), "tp"),
            P(("shard", "ctx"), None),
            P(("shard", "ctx")),
            P(("shard", "ctx")),
            P(("shard", "ctx"), None, "tp"),
            P(("shard", "ctx"), "tp", None),
            P("shard", "ctx", None),
        ),
        out_specs=(
            P("shard", "ctx", None),
            P("shard", "ctx", None),
            P(None, ("shard", "ctx"), "tp"),
            P(("shard", "ctx"), "tp"),
            P(("shard", "ctx"), None),
            P(("shard", "ctx")),
            P(("shard", "ctx")),
            P(("shard", "ctx"), None, "tp"),
            P(("shard", "ctx"), "tp", None),
        ),
        check_vma=False,
    )
```

time: 1560 us -> 600 us (0.38)
  waiting for transfers between devices: 641 us -> 7.98 us
  Pallas kernels: 0 us -> 354 us
  matrix products: 436 us -> 118 us
  blocking collectives: 235 us -> 3 us
  other arithmetic: 100 us -> 32.4 us
  local copies, waits for them, and re-layouts: 103 us -> 46.3 us
    pallas_call x0 -> x10, Pallas kernels: none -> 354 us  [the longest x8 277 us: exchange(): pl.pallas_call(body, name=name, out_shape=tuple(out_shapes), in_specs=[an...]
    dot_general x70 -> x24, matrix products: 432 us -> 118 us  [the longest x9 42.8 us: tn(): lax.dot_general(left, right, (((0,), (0,)), ((), ())), preferred_element_...]
    unnamed x12 -> x4, waiting for transfers between devices: 232 us -> 0.72 us
    reduce_scatter x2 -> x0, waiting for transfers between devices: 167 us -> none  [the longest x1 86 us: local(): lax.psum_scatter(grad_all_pairs.astype(jnp.bfloat16), 'ctx', scatter_dime...]
    all_gather x3 -> x2, waiting for transfers between devices: 105 us -> 0.02 us  [the longest x1 0.02 us: local(): lax.all_gather(by_ctx.transpose(1, 0, 2).reshape(rows, ctxs * 3 * wide),...]
    unnamed x2 -> x0, blocking collectives: 88.6 us -> none
    all_gather x1 -> x0, blocking collectives: 78.6 us -> none  [local(): lax.all_gather(router, ('shard', 'ctx'), axis=0, tiled=True)]
    psum x3 -> x0, waiting for transfers between devices: 69.5 us -> none  [the longest x1 35.1 us: local(): summed = lax.psum(partial_out.astype(jnp.bfloat16), 'tp')]
  transfers between devices with their start and end apart: 13 -> 5, of which waited for: 11 -> 1; matrix products, arithmetic and copies ran while one was open for 17% -> 16% of each run, Pallas kernels for 0% -> 39%
where the time goes in v1:
time: 600 us; the launch traced here: 590 us
  Pallas kernels  354 us (59%)
  matrix products  118 us (20%)
  local copies, waits for them, and re-layouts  46.3 us (8%)
  other arithmetic  32.4 us (5%)
  between operations  15.5 us (3%)
  starting transfers between devices  13 us (2%)
  waiting for transfers between devices  7.98 us (1%)
    pallas_call x8, Pallas kernels, exchange(): pl.pallas_call(body, name=name, out_shape=tuple(out_shapes), in_specs=[an...  277 us
    dot_general x9, matrix products, tn(): lax.dot_general(left, right, (((0,), (0,)), ((), ())), preferred_element_...  42.8 us
    pallas_call x1, Pallas kernels, attention_backward(): pl.pallas_call(functools.partial(backward_kernel, heads, size, blocks), n...  42.5 us
    dot_general x7, matrix products, nt(): lax.dot_general(left, right, (((1,), (1,)), ((), ())), preferred_element_...  37.7 us
    dot_general x8, matrix products, nn(): lax.dot_general(left, right, (((1,), (0,)), ((), ())), preferred_element_...  37.2 us
    pallas_call x1, Pallas kernels, attention_forward(): pl.pallas_call(functools.partial(forward_kernel, heads, size), name='atte...  35.1 us
    unnamed x91, local copies, waits for them, and re-layouts  23.8 us
  transfers between devices with their start and end apart: 5, of which 1 were waited for; matrix products, arithmetic and copies ran while one was open for 16% of the time, Pallas kernels for 39%

profile of v1, /device:TPU:0, one launch (start us, length us, event | category | flops | bytes accessed | tf_op | source)
XLA Modules:
  0.0 590.2 jit_solution(15459277621576178044)
XLA Ops:
  11.1 4.2 fusion.63
  15.4 8.5 %all-to-all-start = ((bf16[16,40,1024]{2,1,0:T(8,128)(2,1)}), bf16[16,40,1024]{2,1,0:T(8,128)(2,1)S(1)}, u32[]{:S(2)}, u32[]{:S(2)}) async-start(bf16[16,40,1024]{2,1,0:T(8,128)(2,1)} %bitcast.147), calls=%async_computation | async-start | bytes 2621440 | tf_op jit(solution)/shard_map/all_to_all | solution.py:493
  36.5 4.6 copy.65
  45.3 73.9 %gather_rows.1 = (bf16[4,2,512,1024]{3,2,1,0:T(8,128)(2,1)}, bf16[16,64,512]{2,1,0:T(8,128)(2,1)}) custom-call(bf16[512,1024]{1,0:T(8,128)(2,1)} %fusion.57.refs_0_, bf16[4,64,512]{2,1,0:T(8,128)(2,1)} %pad_maximum_fusion.refs_1_), custom_call_target="tpu_custom_call" | custom-call | tf_op jit(solution)/shard_map/gather_rows/pallas_call | solution.py:174
  125.8 9.3 %convolution_convert_fusion.q_ref.k_ref.v_ref = bf16[4096,384]{1,0:T(8,128)(2,1)} fusion(bf16[4096,1024]{1,0:T(8,128)(2,1)} %bitcast.168, bf16[1024,512]{1,0:T(8,128)(2,1)S(1)} %bitcast.155), kind=kOutput, calls=%fused_computation.10 | convolution fusion | flops 3222798336 | bytes 12320768 | tf_op jit(solution)/shard_map/dot_general | solution.py:190
  135.1 35.1 %attention_forward.1 = (bf16[4096,128]{1,0:T(8,128)(2,1)}, f32[8,1,1024]{2,1,0:T(1,128)}) custom-call(s32[1]{0:T(128)} %copy.81.len_ref, bf16[4096,384]{1,0:T(8,128)(2,1)} %convolution_convert_fusion.q_ref.k_ref.v_ref, bf16[4096,384]{1,0:T(8,128)(2,1)} %convolution_convert_fusion.q_ref.k_ref.v_ref, bf16[4096,384]{1,0:T(8,128)(2,1)} %convolution_convert_fusion.q_ref.k_ref.v_ref), custom_call_target="tpu_custom_call" | custom-call | flops 34359738368 | bytes 4194304 | tf_op jit(solution)/shard_map/attention_forward/pallas_call | solution.py:253
  171.2 17.7 %mixed_home.1 = (bf16[1024,512]{1,0:T(8,128)(2,1)}, bf16[1024,512]{1,0:T(8,128)(2,1)}, bf16[1024,512]{1,0:T(8,128)(2,1)}, bf16[1024,1536]{1,0:T(8,128)(2,1)}, bf16[16,40,1024]{2,1,0:T(8,128)(2,1)}) custom-call(bf16[4096,128]{1,0:T(8,128)(2,1)} %get-tuple-element.27.refs_0_.o_ref, bf16[1024,512]{1,0:T(8,128)(2,1)} %all-gather.3.cloned.1.call-done.refs_1_, ...), custom_call_target="tpu_custom_call" | custom-call | tf_op jit(solution)/shard_map/mixed_home/pallas_call | solution.py:174
  188.9 3.0 fusion.118
  200.6 54.2 %dispatch.1 = (bf16[2,16,40,1024]{3,2,1,0:T(8,128)(2,1)}, f32[2,16,8,128]{3,2,1,0:T(8,128)}) custom-call(bf16[16,40,1024]{2,1,0:T(8,128)(2,1)} %bitcast.148, f32[16,8,128]{2,1,0:T(8,128)} %broadcast_in_dim.43.refs_1_), custom_call_target="tpu_custom_call" | custom-call | tf_op jit(solution)/shard_map/dispatch/pallas_call | solution.py:174
  255.7 8.4 %fusion.37 = f32[1280,2048]{1,0:T(8,128)S(1)} fusion(bf16[1280,1024]{1,0:T(8,128)(2,1)} %bitcast.170, bf16[1,1024,2048]{2,1,0:T(8,128)(2,1)} %param.19), kind=kOutput, calls=%fused_computation.46 | convolution fusion | flops 5368709120 | bytes 17301504 | tf_op jit(solution)/shard_map/dot_general | solution.py:190
  264.2 7.8 %fusion.43 = bf16[1280,1024]{1,0:T(8,128)(2,1)} fusion(bf16[1,2048,1024]{2,1,0:T(8,128)(2,1)S(1)} %copy-done.34, f32[1280,2048]{1,0:T(8,128)S(1)} %fusion.37), kind=kOutput, calls=%fused_computation.61 | convolution fusion | flops 5393612800 | bytes 17301504 | tf_op jit(solution)/shard_map/dot_general | solution.py:190
  272.5 14.2 %fusion.6 = bf16[1280,2048]{1,0:T(8,128)(2,1)S(1)} fusion(f32[1280,2048]{1,0:T(8,128)} %copy-done.40, bf16[1280,1024]{1,0:T(8,128)(2,1)S(1)} %bitcast.141, bf16[1,2048,1024]{2,1,0:T(8,128)(2,1)S(1)} %copy-done.34), kind=kOutput, calls=%fused_computation.8 | convolution fusion | flops 5421137920 | bytes 22544384 | tf_op jit(solution)/shard_map/dot_general | solution.py:186
  286.7 7.1 %fusion.40 = bf16[1280,1024]{1,0:T(8,128)(2,1)} fusion(bf16[1280,2048]{1,0:T(8,128)(2,1)S(1)} %fusion.6, bf16[1,1024,2048]{2,1,0:T(8,128)(2,1)S(1)} %copy-done.35), kind=kOutput, calls=%fused_computation.60 | convolution fusion | flops 5370019840 | bytes 12058624 | tf_op jit(solution)/shard_map/dot_general | solution.py:186
  293.8 8.1 %convolution_bitcast_fusion.1 = f32[1,1024,2048]{2,1,0:T(8,128)} fusion(bf16[1280,1024]{1,0:T(8,128)(2,1)S(1)} %bitcast.171, bf16[1280,2048]{1,0:T(8,128)(2,1)S(1)} %fusion.6), kind=kOutput, calls=%fused_computation.32 | convolution fusion | flops 5368709120 | bytes 16252928 | tf_op jit(solution)/shard_map/dot_general | solution.py:194
  304.4 3.4 sum_out.1
  307.9 3.3 fusion.52
  311.2 4.4 all-to-all-start.1
  318.1 3.4 sum_grad.1
  326.6 11.6 %convolution_bitcast_fusion = f32[1,2048,1024]{2,1,0:T(8,128)} fusion(bf16[1280,1024]{1,0:T(8,128)(2,1)S(1)} %fusion.17, f32[1280,2048]{1,0:T(8,128)} %copy-done.40), kind=kOutput, calls=%fused_computation.31 | convolution fusion | flops 5392302080 | bytes 21495808 | tf_op jit(solution)/shard_map/dot_general | solution.py:194
  338.1 7.2 %all-to-all-done.1.refs_1_ = bf16[16,40,1024]{2,1,0:T(8,128)(2,1)} async-done(((bf16[16,40,1024]{2,1,0:T(8,128)(2,1)}), bf16[16,40,1024]{2,1,0:T(8,128)(2,1)}, u32[]{:S(2)}, u32[]{:S(2)}) %all-to-all-start.1) | async-done | bytes 1310752 | tf_op jit(solution)/shard_map/all_to_all | solution.py:576
  345.4 28.8 %grad_home.1 = (bf16[2,16,40,1024]{3,2,1,0:T(8,128)(2,1)}, bf16[16,40,1024]{2,1,0:T(8,128)(2,1)}) custom-call(bf16[16,40,1024]{2,1,0:T(8,128)(2,1)} %fusion.51.refs_0_, bf16[16,40,1024]{2,1,0:T(8,128)(2,1)} %all-to-all-done.1.refs_1_), custom_call_target="tpu_custom_call" | custom-call | tf_op jit(solution)/shard_map/grad_home/pallas_call | solution.py:174
  378.2 3.5 fusion.9
  389.9 3.9 multiply_add_fusion
  398.9 19.4 %grad_mixed.1.do_ref = bf16[4096,128]{1,0:T(8,128)(2,1)} custom-call(bf16[1024,512]{1,0:T(8,128)(2,1)} %convolution_convert_fusion.1.refs_0_), custom_call_target="tpu_custom_call" | custom-call | tf_op jit(solution)/shard_map/grad_mixed/pallas_call | solution.py:174
  422.3 42.5 %attention_backward.1.refs_0_ = bf16[4096,384]{1,0:T(8,128)(2,1)} custom-call(s32[1]{0:T(128)} %copy.81.len_ref, bf16[4096,384]{1,0:T(8,128)(2,1)} %convolution_convert_fusion.q_ref.k_ref.v_ref, bf16[4096,384]{1,0:T(8,128)(2,1)} %convolution_convert_fusion.q_ref.k_ref.v_ref, bf16[4096,384]{1,0:T(8,128)(2,1)} %convolution_convert_fusion.q_ref.k_ref.v_ref, ...), custom_call_target="tpu_custom_call" | custom-call | flops 85899345920 | bytes 8388608 | tf_op jit(solution)/shard_map/attention_backward/pallas_call | solution.py:361
  467.3 9.8 %convolution_convert_fusion.2 = bf16[1024,384]{1,0:T(8,128)(2,1)} fusion(bf16[4096,1024]{1,0:T(8,128)(2,1)} %bitcast.169, bf16[4096,384]{1,0:T(8,128)(2,1)} %attention_backward.1.refs_0_), kind=kOutput, calls=%fused_computation.88 | convolution fusion | flops 3221618688 | bytes 12320768 | tf_op jit(solution)/shard_map/dot_general | solution.py:194
  477.2 76.1 %grad_projected.1 = (bf16[1024,1536]{1,0:T(8,128)(2,1)}, bf16[1024,1536]{1,0:T(8,128)(2,1)}, bf16[16,64,384]{2,1,0:T(8,128)(2,1)}) custom-call(bf16[4096,384]{1,0:T(8,128)(2,1)} %attention_backward.1.refs_0_, bf16[16,64,384]{2,1,0:T(8,128)(2,1)} %bitcast.151), custom_call_target="tpu_custom_call" | custom-call | tf_op jit(solution)/shard_map/grad_projected/pallas_call | solution.py:174
  553.3 5.5 fusion.119
  558.8 3.8 fusion.113
  562.7 3.6 fusion.26
  566.3 5.3 copy.69
  576.1 3.0 psum.7
  (171 shorter events, 80.3 us)
Async XLA Ops:
  7.2 162.9 %all-gather.3.cloned.1.call-start = ((), (), s32[]{:S(2)}) async-start(), calls=%async_computation.3 | async-start | bytes 1114112 | tf_op jit(solution)/shard_map/all_gather | solution.py:447
  11.1 12.8 %copy-start.39 = (bf16[64]{0:T(256)(128)(2,1)S(1)}, bf16[64]{0:T(256)(128)(2,1)}, u32[]{:S(2)}) copy-start(bf16[64]{0:T(256)(128)(2,1)} %param.17) | copy-start | bytes 388
  15.4 17.2 %copy-start.9 = (bf16[1,1024,1024]{2,1,0:T(8,128)(2,1)S(1)}, bf16[1,1024,1024]{2,1,0:T(8,128)(2,1)}, u32[]{:S(2)}) copy-start(bf16[1,1024,1024]{2,1,0:T(8,128)(2,1)} %param.11) | copy-start | bytes 6291460
  15.4 17.8 %copy-start.30 = (bf16[64,16]{0,1:T(8,128)(2,1)S(1)}, bf16[64,16]{0,1:T(8,128)(2,1)}, u32[]{:S(2)}) copy-start(bf16[64,16]{0,1:T(8,128)(2,1)} %param.16) | copy-start | bytes 6148
  15.4 17.9 %copy-start.33 = (bf16[64]{0:T(256)(128)(2,1)S(1)}, bf16[64]{0:T(256)(128)(2,1)}, u32[]{:S(2)}) copy-start(bf16[64]{0:T(256)(128)(2,1)} %param.18) | copy-start | bytes 388
  15.4 154.8 %all-to-all-start = ((bf16[16,40,1024]{2,1,0:T(8,128)(2,1)}), bf16[16,40,1024]{2,1,0:T(8,128)(2,1)S(1)}, u32[]{:S(2)}, u32[]{:S(2)}) async-start(bf16[16,40,1024]{2,1,0:T(8,128)(2,1)} %bitcast.147), calls=%async_computation | async-start | bytes 2621440 | tf_op jit(solution)/shard_map/all_to_all | solution.py:493
  23.8 146.3 %all-gather.5.cloned.1.call-start = ((), (), s32[]{:S(2)}) async-start(), calls=%async_computation.4 | async-start | bytes 3342336 | tf_op jit(solution)/shard_map/all_gather | solution.py:444
  23.9 12.6 %copy-start.31 = (f32[64]{0:T(128)}, f32[64]{0:T(128)S(1)}, u32[]{:S(2)}) copy-start(f32[64]{0:T(128)S(1)} %convert_element_type.175) | copy-start | bytes 772
  36.5 155.4 %copy-start.2 = (bf16[1,1024,1024]{1,2,0:T(8,128)(2,1)}, bf16[1,1024,1024]{1,2,0:T(8,128)(2,1)S(1)}, u32[]{:S(2)}) copy-start(bf16[1,1024,1024]{1,2,0:T(8,128)(2,1)S(1)} %copy.60) | copy-start | bytes 6291460
  124.6 10.5 %copy-start.25 = (f32[1024]{0:T(1024)}, f32[1024]{0:T(1024)S(1)}, u32[]{:S(2)}) copy-start(f32[1024]{0:T(1024)S(1)} %broadcast_multiply_fusion.3) | copy-start | bytes 12292
  255.7 8.4 %copy-start.34 = (bf16[1,2048,1024]{2,1,0:T(8,128)(2,1)S(1)}, bf16[1,2048,1024]{2,1,0:T(8,128)(2,1)}, u32[]{:S(2)}) copy-start(bf16[1,2048,1024]{2,1,0:T(8,128)(2,1)} %param.20) | copy-start | bytes 12582916
  264.1 7.8 %copy-start.40 = (f32[1280,2048]{1,0:T(8,128)}, f32[1280,2048]{1,0:T(8,128)S(1)}, u32[]{:S(2)}) copy-start(f32[1280,2048]{1,0:T(8,128)S(1)} %fusion.37) | copy-start | bytes 31457284
  264.1 7.8 %copy-start.8 = (bf16[16,40,1024]{2,1,0:T(8,128)(2,1)S(1)}, bf16[16,40,1024]{2,1,0:T(8,128)(2,1)}, u32[]{:S(2)}) copy-start(bf16[16,40,1024]{2,1,0:T(8,128)(2,1)} %copy-done.7) | copy-start | bytes 3932164
  264.1 7.8 %copy-start.13 = (bf16[16,40,1024]{2,1,0:T(8,128)(2,1)S(1)}, bf16[16,40,1024]{2,1,0:T(8,128)(2,1)}, u32[]{:S(2)}) copy-start(bf16[16,40,1024]{2,1,0:T(8,128)(2,1)} %get-tuple-element.33) | copy-start | bytes 3932164
  272.5 14.2 %copy-start.35 = (bf16[1,1024,2048]{2,1,0:T(8,128)(2,1)S(1)}, bf16[1,1024,2048]{2,1,0:T(8,128)(2,1)}, u32[]{:S(2)}) copy-start(bf16[1,1024,2048]{2,1,0:T(8,128)(2,1)} %param.19) | copy-start | bytes 12582916
  286.7 7.1 %copy-start.38 = (bf16[2,16,40,1024]{3,2,1,0:T(8,128)(2,1)S(1)}, bf16[2,16,40,1024]{3,2,1,0:T(8,128)(2,1)}, u32[]{:S(2)}) copy-start(bf16[2,16,40,1024]{3,2,1,0:T(8,128)(2,1)} %get-tuple-element.31) | copy-start | bytes 7864324
  311.2 34.2 %all-to-all-start.1 = ((bf16[16,40,1024]{2,1,0:T(8,128)(2,1)}), bf16[16,40,1024]{2,1,0:T(8,128)(2,1)}, u32[]{:S(2)}, u32[]{:S(2)}) async-start(bf16[16,40,1024]{2,1,0:T(8,128)(2,1)} %fusion.52), calls=%async_computation.1 | async-start | bytes 2621440 | tf_op jit(solution)/shard_map/all_to_all | solution.py:576
  315.6 263.4 %reduce-scatter.4.cloned.1.call-start = ((), (), s32[]{:S(2)}) async-start(), calls=%async_computation.5 | async-start | bytes 2785280
  378.2 3.5 copy-start.6
  378.2 3.5 copy-start.18
  378.2 3.5 copy-start.22
  378.2 3.5 copy-start.24
  389.9 3.9 copy-start.11
  396.6 21.6 %copy-start.27 = (f32[640]{0:T(1024)S(1)}, f32[640]{0:T(1024)}, u32[]{:S(2)}) copy-start(f32[640]{0:T(1024)} %pad.8.clone) | copy-start | bytes 7684
  422.3 42.5 %copy-start.10 = (bf16[1,1024,1024]{1,2,0:T(8,128)(2,1)S(1)}, bf16[1,1024,1024]{1,2,0:T(8,128)(2,1)}, u32[]{:S(2)}) copy-start(bf16[1,1024,1024]{1,2,0:T(8,128)(2,1)} %get-tuple-element.94) | copy-start | bytes 6291460
  467.3 85.9 %copy-start.17 = (bf16[1024,1536]{1,0:T(8,128)(2,1)S(1)}, bf16[1024,1536]{1,0:T(8,128)(2,1)}, u32[]{:S(2)}) copy-start(bf16[1024,1536]{1,0:T(8,128)(2,1)} %all-gather.5.cloned.1.call-done.refs_2_) | copy-start | bytes 9437188
  553.2 5.5 copy-start.3
  553.3 5.5 copy-start.26
  553.3 5.5 copy-start.28
  553.3 5.5 copy-start.36
  553.3 5.5 copy-start.37
  558.8 3.9 copy-start.5
  (14 other events, 35.5 us)
Sparse Core Ops, SparseCore 0:
  10.7 90.2 all-gather.2
  103.8 65.9 all-gather.4
  422.4 91.1 reduce-scatter.3

commit v2 on v1

--- a/solution.py
+++ b/solution.py
@@ -208,50 +208,61 @@
     return total
 
 
-def forward_kernel(heads, size, len_ref, q_ref, k_ref, v_ref, o_ref, lse_ref):
+def forward_kernel(heads, size, span, spans, len_ref, q_ref, k_ref, v_ref, o_ref, lse_ref, turned):
     i = pl.program_id(0)
     length = len_ref[0]
     scale = HEAD_DIM ** (-0.5)
+    tall = heads * size
+    wide = heads * HEAD_DIM
+
+    @pl.when(i == 0)
+    def _():
+        def turn(j, carry):
+            place = pl.ds(pl.multiple_of(j * span, span), span)
+            turned[j] = jnp.transpose(v_ref[place, :].astype(F32)).astype(BF16)
+            return carry
+
+        lax.fori_loop(0, spans, turn, 0)
+
     queries = stacked((q_ref[...].astype(F32) * scale).astype(BF16), heads)
-    tall = heads * size
-    row = lax.broadcasted_iota(jnp.int32, (tall, 1), 0) % size
-    limit = jnp.minimum(i * size + row, length - 1)
-    full = (jnp.minimum(i * size, length - 1) + 1) // size
-    every = (jnp.minimum((i + 1) * size, length) + size - 1) // size
+    inner = lax.broadcasted_iota(jnp.int32, (1, tall), 1) % size
+    limit = jnp.minimum(i * size + inner, length - 1)
+    full = (jnp.minimum(i * size, length - 1) + 1) // span
+    every = (jnp.minimum((i + 1) * size, length) + span - 1) // span
 
     def step(masked, j, state):
         top, total, accum = state
-        place = pl.ds(pl.multiple_of(j * size, size), size)
-        scores = nt(queries, k_ref[place, :]) * LOG2E
+        place = pl.ds(pl.multiple_of(j * span, span), span)
+        scores = nt(k_ref[place, :], queries) * LOG2E
         if masked:
-            column = j * size + lax.broadcasted_iota(jnp.int32, (tall, size), 1)
+            column = j * span + lax.broadcasted_iota(jnp.int32, (span, tall), 0)
             scores = jnp.where(column <= limit, scores, MASKED)
-        new_top = jnp.maximum(top, jnp.max(scores, axis=-1, keepdims=True))
+        new_top = jnp.maximum(top, jnp.max(scores, axis=0, keepdims=True))
         factor = jnp.exp2(top - new_top)
         weights = jnp.exp2(scores - new_top)
-        total = total * factor + jnp.sum(weights, axis=-1, keepdims=True)
-        accum = accum * factor + nn(weights.astype(BF16), v_ref[place, :])
+        total = total * factor + jnp.sum(weights, axis=0, keepdims=True)
+        accum = accum * factor + nn(turned[j], weights.astype(BF16))
         return new_top, total, accum
 
     state = (
-        jnp.full((tall, 1), MASKED, F32),
-        jnp.zeros((tall, 1), F32),
-        jnp.zeros((tall, heads * HEAD_DIM), F32),
+        jnp.full((1, tall), MASKED, F32),
+        jnp.zeros((1, tall), F32),
+        jnp.zeros((wide, tall), F32),
     )
     state = lax.fori_loop(0, full, functools.partial(step, False), state)
     top, total, accum = lax.fori_loop(full, every, functools.partial(step, True), state)
-    o_ref[...] = merged(accum / total, heads).astype(BF16)
-    log_total = jnp.broadcast_to(top + jnp.log2(total), (tall, 128))
-    lse_ref[0] = jnp.transpose(log_total)[:1, :]
+    o_ref[...] = merged(jnp.transpose(accum / total), heads).astype(BF16)
+    lse_ref[0] = top + jnp.log2(total)
 
 
 def attention_forward(projected, lengths, heads):
     count, _ = projected.shape
     wide = heads * HEAD_DIM
     size = BLOCK
+    span = 2 * BLOCK
     blocks = count // size
     return pl.pallas_call(
-        functools.partial(forward_kernel, heads, size),
+        functools.partial(forward_kernel, heads, size, span, count // span),
         name="attention_forward",
         out_shape=(
             jax.ShapeDtypeStruct((count, wide), BF16),
@@ -269,6 +280,7 @@
                 pl.BlockSpec((size, wide), lambda i, n: (i, 0)),
                 pl.BlockSpec((1, 1, heads * size), lambda i, n: (i, 0, 0)),
             ],
+            scratch_shapes=[pltpu.VMEM((count // span, wide, span), BF16)],
         ),
         cost_estimate=pl.CostEstimate(
             flops=16 * count * count * wide,
@@ -389,6 +401,49 @@
     )(lengths, projected, projected, projected, mixed, grad_mixed, lse)
 
 
+def pair_sum(name, collective_id, partial):
+    shape = partial.shape[1:]
+
+    def body(in_ref, out_ref, own, got, sems):
+        other = {"tp": 1 - lax.axis_index("tp")}
+        barrier = pltpu.get_barrier_semaphore()
+        pl.semaphore_signal(barrier, inc=1, device_id=other, device_id_type=MESH)
+        pl.semaphore_wait(barrier, 1)
+        away = pltpu.make_async_remote_copy(
+            src_ref=in_ref.at[1],
+            dst_ref=got,
+            send_sem=sems.at[0],
+            recv_sem=sems.at[1],
+            device_id=other,
+            device_id_type=MESH,
+        )
+        away.start()
+        here = pltpu.make_async_copy(in_ref.at[0], own, sems.at[2])
+        here.start()
+        here.wait()
+        away.wait()
+
+        def add(e, carry):
+            out_ref[e] = (own[e].astype(F32) + got[e].astype(F32)).astype(BF16)
+            return carry
+
+        lax.fori_loop(0, shape[0], add, 0)
+
+    return pl.pallas_call(
+        body,
+        name=name,
+        out_shape=jax.ShapeDtypeStruct(shape, BF16),
+        in_specs=[pl.BlockSpec(memory_space=pl.ANY)],
+        out_specs=pl.BlockSpec(memory_space=pltpu.VMEM),
+        scratch_shapes=[
+            pltpu.VMEM(shape, BF16),
+            pltpu.VMEM(shape, BF16),
+            pltpu.SemaphoreType.DMA((3,)),
+        ],
+        compiler_params=pltpu.CompilerParams(collective_id=collective_id, has_side_effects=True),
+    )(partial)
+
+
 def normed(values):
     center = values - jnp.mean(values, axis=-1, keepdims=True)
     inverse = lax.rsqrt(jnp.mean(center * center, axis=-1, keepdims=True) + EPSILON)
@@ -405,6 +460,244 @@
 
 def shape_of(extent, dtype):
     return jax.ShapeDtypeStruct(extent, dtype)
+
+
+def prepare_kernel(experts, ctxs, wide, where_ref, tokens_ref, weight_ref, small_ref, unit_ref, sent_ref, rows_ref):
+    unit_ref[...] = normed(tokens_ref[...].astype(F32))[0].astype(BF16)
+    gain = small_ref[:, experts + 1 : experts + 2].astype(F32)
+    for k in range(3):
+        scaled = (weight_ref[k].astype(F32) * gain).astype(BF16)
+        for c in range(ctxs):
+            piece = scaled[:, c * wide : (c + 1) * wide]
+            sent_ref[c, :, k * wide : (k + 1) * wide] = piece
+            rows_ref[:, (3 * c + k) * wide : (3 * c + k + 1) * wide] = piece
+    for c in range(ctxs):
+        sent_ref[c, :, 3 * wide :] = small_ref[...]
+
+
+def prepare(tokens, weight_qkv, small, tp_rank, half, ctxs, wide, experts):
+    _, rows, head_width = weight_qkv.shape
+    width = tokens.shape[1]
+    pad = small.shape[1]
+    return pl.pallas_call(
+        functools.partial(prepare_kernel, experts, ctxs, wide),
+        name="prepare",
+        out_shape=(
+            shape_of((half, width), BF16),
+            shape_of((ctxs, rows, 3 * wide + pad), BF16),
+            shape_of((rows, 3 * head_width), BF16),
+        ),
+        grid_spec=pltpu.PrefetchScalarGridSpec(
+            num_scalar_prefetch=1,
+            grid=(1,),
+            in_specs=[
+                pl.BlockSpec((half, width), lambda i, w: (w[0], 0)),
+                pl.BlockSpec(weight_qkv.shape, lambda i, w: (0, 0, 0)),
+                pl.BlockSpec(small.shape, lambda i, w: (0, 0)),
+            ],
+            out_specs=[
+                pl.BlockSpec((half, width), lambda i, w: (0, 0)),
+                pl.BlockSpec((ctxs, rows, 3 * wide + pad), lambda i, w: (0, 0, 0)),
+                pl.BlockSpec((rows, 3 * head_width), lambda i, w: (0, 0)),
+            ],
+        ),
+    )(tp_rank, tokens, weight_qkv, small)
+
+
+def middle_kernel(
+    experts, tokens_ref, own_ref, par_ref, proj_own_ref, proj_par_ref, gain_ref, router_ref, route_ref,
+    middle_ref, second_ref, probs_ref, gate_ref,
+):
+    branch = nt(own_ref[...], proj_own_ref[...]) + nt(par_ref[...], proj_par_ref[...])
+    middle = tokens_ref[...].astype(F32) + branch
+    middle_ref[...] = middle
+    second = (normed(middle)[0] * gain_ref[...].astype(F32)).astype(BF16)
+    second_ref[...] = second
+    logits = nn(second, router_ref[...])
+    lane = lax.broadcasted_iota(jnp.int32, logits.shape, 1)
+    logits = jnp.where(lane < experts, logits, MASKED)
+    powers = jnp.exp(logits - jnp.max(logits, axis=-1, keepdims=True))
+    powers = jnp.where(lane < experts, powers, 0.0)
+    probs = powers / jnp.sum(powers, axis=-1, keepdims=True)
+    probs_ref[...] = probs
+    gate_ref[...] = jnp.sum(jnp.where(lane == route_ref[...], probs, 0.0), axis=-1, keepdims=True)
+
+
+ROWS = 256
+
+
+def middle_step(tokens, own, par, proj_own, proj_par, gain, router, route, experts):
+    count, width = tokens.shape
+    features = own.shape[1]
+    pad = router.shape[1]
+    tile = min(ROWS, count)
+
+    def rows(extent):
+        return pl.BlockSpec((tile, extent), lambda i: (i, 0))
+
+    def whole(array):
+        return pl.BlockSpec(array.shape, lambda i: (0, 0))
+
+    return pl.pallas_call(
+        functools.partial(middle_kernel, experts),
+        name="middle_step",
+        grid=(count // tile,),
+        out_shape=(
+            shape_of((count, width), F32),
+            shape_of((count, width), BF16),
+            shape_of((count, pad), F32),
+            shape_of((count, 1), F32),
+        ),
+        in_specs=[
+            rows(width), rows(features), rows(features), whole(proj_own), whole(proj_par),
+            whole(gain), whole(router), rows(1),
+        ],
+        out_specs=[rows(width), rows(width), rows(pad), rows(1)],
+    )(tokens, own, par, proj_own, proj_par, gain, router, route)
+
+
+def home_kernel(
+    experts, limit, where_ref, cot_ref, middle_ref, second_ref, probs_ref, gate_ref, route_ref, target_ref,
+    own_slot_ref, par_slot_ref, back_own_ref, back_par_ref, grad_ref, gain_ref, router_ref, proj_ref,
+    output_ref, grad_middle_ref, grad_branch_ref, grad_mixed_ref, grad_logits_ref, grad_gain_ref,
+):
+    i = pl.program_id(0)
+    tile, width = cot_ref.shape
+    target = target_ref[...]
+    pick_own = (target == own_slot_ref[...]).astype(F32).astype(BF16)
+    pick_par = (target == par_slot_ref[...]).astype(F32).astype(BF16)
+    fetched = nn(pick_own, back_own_ref[...]) + nn(pick_par, back_par_ref[...])
+    grad_home = nn(pick_own, grad_ref[0]) + nn(pick_par, grad_ref[1])
+    place = where_ref[0] + i * tile + lax.broadcasted_iota(jnp.int32, (tile, 1), 0)
+    valid = (place < where_ref[1]).astype(F32)
+    kept = (target < limit).astype(F32)
+    gate = gate_ref[...]
+    probs = probs_ref[...]
+    middle = middle_ref[...]
+    output_ref[...] = (valid * (middle + (kept * gate) * fetched)).astype(BF16)
+    grad_out = valid * cot_ref[...].astype(F32)
+    grad_gate = kept * jnp.sum(grad_out * fetched, axis=-1, keepdims=True)
+    lane = lax.broadcasted_iota(jnp.int32, probs.shape, 1)
+    hot = (lane == route_ref[...]).astype(F32)
+    grad_logits = ((grad_gate * gate) * (hot - probs)).astype(BF16)
+    grad_logits_ref[...] = grad_logits
+    gain = gain_ref[...].astype(F32)
+    unit, inverse = normed(middle)
+    grad_second = grad_home + nt(grad_logits, router_ref[...])
+    grad_gain = jnp.sum(grad_second * unit, axis=0, keepdims=True)
+
+    @pl.when(i == 0)
+    def _():
+        grad_gain_ref[...] = grad_gain
+
+    @pl.when(i > 0)
+    def _():
+        grad_gain_ref[...] += grad_gain
+
+    grad_middle = grad_out + norm_back(grad_second * gain, unit, inverse)
+    grad_middle_ref[...] = grad_middle
+    grad_branch = grad_middle.astype(BF16)
+    grad_branch_ref[...] = grad_branch
+    grad_mixed_ref[...] = nn(grad_branch, proj_ref[...]).astype(BF16)
+
+
+def home_step(
+    cot, middle, second, probs, gate, route, target, own_slot, par_slot, back_own, back_par, grads,
+    gain, router, proj, where, experts, limit,
+):
+    count, width = cot.shape
+    features = proj.shape[1]
+    pad = router.shape[1]
+    tile = min(ROWS, count)
+
+    def rows(extent):
+        return pl.BlockSpec((tile, extent), lambda i, w: (i, 0))
+
+    def whole(array):
+        return pl.BlockSpec(array.shape, lambda i, w: (0,) * array.ndim)
+
+    return pl.pallas_call(
+        functools.partial(home_kernel, experts, limit),
+        name="home_step",
+        out_shape=(
+            shape_of((count, width), BF16),
+            shape_of((count, width), F32),
+            shape_of((count, width), BF16),
+            shape_of((count, features), BF16),
+            shape_of((count, pad), BF16),
+            shape_of((1, width), F32),
+        ),
+        grid_spec=pltpu.PrefetchScalarGridSpec(
+            num_scalar_prefetch=1,
+            grid=(count // tile,),
+            in_specs=[
+                rows(width), rows(width), rows(width), rows(pad), rows(1), rows(1), rows(1),
+                whole(own_slot), whole(par_slot), whole(back_own), whole(back_par), whole(grads),
+                whole(gain), whole(router), whole(proj),
+            ],
+            out_specs=[
+                rows(width), rows(width), rows(width), rows(features), rows(pad),
+                pl.BlockSpec((1, width), lambda i, w: (0, 0)),
+            ],
+        ),
+    )(
+        where, cot, middle, second, probs, gate, route, target, own_slot, par_slot, back_own, back_par,
+        grads, gain, router, proj,
+    )
+
+
+def last_kernel(tokens_ref, grad_middle_ref, own_ref, par_ref, weight_own_ref, weight_par_ref, out_ref):
+    ctxs, _, piece = own_ref.shape
+    scaled = None
+    for got, weight in ((own_ref, weight_own_ref), (par_ref, weight_par_ref)):
+        for c in range(ctxs):
+            part = nt(got[c], weight[:, c * piece : (c + 1) * piece])
+            scaled = part if scaled is None else scaled + part
+    unit, inverse = normed(tokens_ref[...].astype(F32))
+    out_ref[...] = grad_middle_ref[...] + norm_back(scaled, unit, inverse)
+
+
+def last_step(tokens, grad_middle, own, par, weight_own, weight_par):
+    count, width = tokens.shape
+    ctxs, _, piece = own.shape
+    tile = min(ROWS, count)
+    rows = pl.BlockSpec((tile, width), lambda i: (i, 0))
+    got = pl.BlockSpec((ctxs, tile, piece), lambda i: (0, i, 0))
+    weight = pl.BlockSpec(weight_own.shape, lambda i: (0, 0))
+    return pl.pallas_call(
+        last_kernel,
+        name="last_step",
+        grid=(count // tile,),
+        out_shape=shape_of((count, width), F32),
+        in_specs=[rows, rows, got, got, weight, weight],
+        out_specs=rows,
+    )(tokens, grad_middle, own, par, weight_own, weight_par)
+
+
+def owner_kernel(shards, ctxs, wide, got_ref, weight_ref, gain_ref, grad_ref, sum_ref):
+    gain = gain_ref[...].astype(F32)
+    total = jnp.zeros((got_ref.shape[1], 1), F32)
+    for c in range(ctxs):
+        raw = got_ref[c].astype(F32)
+        for s in range(1, shards):
+            raw = raw + got_ref[s * ctxs + c].astype(F32)
+        for k in range(3):
+            piece = raw[:, k * wide : (k + 1) * wide]
+            grad_ref[k, :, c * wide : (c + 1) * wide] = piece * gain
+            weight = weight_ref[k, :, c * wide : (c + 1) * wide].astype(F32)
+            total = total + jnp.sum(piece * weight, axis=-1, keepdims=True)
+    sum_ref[...] = jnp.broadcast_to(total, sum_ref.shape)
+
+
+def owner_step(got, weight_qkv, gain, shards, ctxs, wide):
+    rows = weight_qkv.shape[1]
+    return pl.pallas_call(
+        functools.partial(owner_kernel, shards, ctxs, wide),
+        name="owner_step",
+        out_shape=(shape_of(weight_qkv.shape, F32), shape_of((rows, 128), F32)),
+        in_specs=[pl.BlockSpec(memory_space=pltpu.VMEM)] * 3,
+        out_specs=(pl.BlockSpec(memory_space=pltpu.VMEM),) * 2,
+    )(got, weight_qkv, gain)
 
 
 def local(
@@ -428,24 +721,17 @@
     length_all = ctxs * count
     ctx_rank = lax.axis_index("ctx")
     tp_rank = lax.axis_index("tp")
-
-    inputs = tokens[0].astype(F32)
-    own_half = lax.dynamic_slice_in_dim(tokens[0], tp_rank * half, half, 0).astype(F32)
-    unit_half = normed(own_half)[0].astype(BF16)
-    scaled_qkv = (weight_qkv.astype(F32) * gain_one.astype(F32)[None, :, None]).astype(BF16)
-    by_ctx = scaled_qkv.reshape(3, rows, ctxs, wide).transpose(2, 1, 0, 3).reshape(ctxs, rows, 3 * wide)
-    pad = -(-(experts + 1) // 128) * 128
+    rows_in = tokens[0]
+    cot = cotangent[0]
+
+    pad = -(-(experts + 2) // 128) * 128
     small = jnp.concatenate(
-        [router, gain_two[:, None], jnp.zeros((rows, pad - experts - 1), BF16)], axis=1
-    )
-    sent_weights = jnp.concatenate(
-        [by_ctx, jnp.broadcast_to(small[None], (ctxs, rows, pad))], axis=2
-    )
-    whole_qkv = lax.all_gather(
-        by_ctx.transpose(1, 0, 2).reshape(rows, ctxs * 3 * wide), group, axis=0, tiled=True
-    )
-    whole_proj = lax.all_gather(weight_proj, group, axis=0, tiled=True)
-
+        [router, gain_two[:, None], gain_one[:, None], jnp.zeros((rows, pad - experts - 2), BF16)],
+        axis=1,
+    )
+    unit_half, sent_weights, row_weights = prepare(
+        rows_in, weight_qkv, small, tp_rank.astype(jnp.int32)[None], half, ctxs, wide, experts
+    )
     unit_all, got_weights = exchange(
         "gather_rows", 1, sizes,
         [
@@ -464,11 +750,16 @@
             ),
         ],
     )
+    unit_all, got_weights, row_weights, weight_late, routes, cot_late = lax.optimization_barrier(
+        (unit_all, got_weights, row_weights, weight_proj, routes, cot)
+    )
+    whole_qkv = lax.all_gather(row_weights, group, axis=0, tiled=True)
+    whole_proj = lax.all_gather(weight_late, group, axis=0, tiled=True)
     unit_all = unit_all.reshape(length_all, width)
     got_weights = got_weights.reshape(width, 3 * wide + pad)
     own_qkv = got_weights[:, : 3 * wide]
-    full_router = got_weights[:, 3 * wide : 3 * wide + experts]
-    full_two = got_weights[:, 3 * wide + experts].astype(F32)
+    full_small = got_weights[:, 3 * wide :]
+    full_two = got_weights[:, 3 * wide + experts].reshape(1, width)
 
     places = ctx_rank * count + jnp.arange(count, dtype=jnp.int32)
     route = routes.reshape(count)
@@ -485,17 +776,22 @@
     slot = (slot // half_cap) * capacity + slot % half_cap
     own_slot = slot + tp_rank * half_cap
     par_slot = slot + (1 - tp_rank) * half_cap
-    pick_own = (own_slot[:, None] == target[None, :]).astype(BF16)
-    pick_par = (par_slot[:, None] == target[None, :]).astype(BF16)
-
-    cot = cotangent[0]
-    sent_cot = nn(pick_own, cot).astype(BF16).reshape(experts, half_cap, width)
+    picked = own_slot[:, None] == target[None, :]
+    pick_own = picked.astype(BF16)
+
+    sent_cot = nn(pick_own, cot_late).astype(BF16).reshape(experts, half_cap, width)
     got_cot = lax.all_to_all(sent_cot, group, split_axis=0, concat_axis=0, tiled=True)
 
     projected = nn(unit_all, own_qkv).astype(BF16)
     mixed_heads, lse = attention_forward(projected, lengths, heads)
 
-    mixed_own, mixed_par, proj_par, qkv_par, cot_par = exchange(
+    def passed(array):
+        return Item(
+            "pair", array, [shape_of(array.shape, BF16)],
+            lambda ref, p: ref, None, relay=lambda ref, q, t: ref, keep=False,
+        )
+
+    mixed_own, mixed_par, proj_par, qkv_par = exchange(
         "mixed_home", 2, sizes,
         [
             Item(
@@ -506,56 +802,39 @@
                 relay=lambda ref, q, t: ref.at[:, pl.ds(pl.multiple_of(q * wide, wide), wide)],
                 block=(count, wide),
             ),
-            Item(
-                "pair", whole_proj, [shape_of(whole_proj.shape, BF16)],
-                lambda ref, p: ref, None, relay=lambda ref, q, t: ref, keep=False,
-            ),
-            Item(
-                "pair", whole_qkv, [shape_of(whole_qkv.shape, BF16)],
-                lambda ref, p: ref, None, relay=lambda ref, q, t: ref, keep=False,
-            ),
-            Item(
-                "pair", got_cot, [shape_of(got_cot.shape, BF16)],
-                lambda ref, p: ref, None, relay=lambda ref, q, t: ref, keep=False,
-            ),
+            passed(whole_proj),
+            passed(whole_qkv),
         ],
     )
 
-    middle = inputs + nt(mixed_own, whole_proj) + nt(mixed_par, proj_par)
-    unit_two, inverse_two = normed(middle)
-    second = (unit_two * full_two).astype(BF16)
-    probs = jax.nn.softmax(nn(second, full_router), axis=-1)
-    gate = jnp.sum(jnp.where(route_hot, probs, 0.0), axis=1)
+    route_column = routes.reshape(count, 1)
+    middle, second, probs, gate = middle_step(
+        rows_in, mixed_own, mixed_par, whole_proj, proj_par, full_two, full_small, route_column, experts
+    )
     sent_rows = nn(pick_own, second).astype(BF16).reshape(experts, half_cap, width)
-    gate_rows = jnp.sum(
-        jnp.where(own_slot[:, None] == target[None, :], gate[None, :], 0.0), axis=1
-    ).reshape(experts, half_cap)
+    gate_rows = jnp.sum(jnp.where(picked, gate.reshape(1, count), 0.0), axis=1)
+    gate_rows = gate_rows.reshape(experts, half_cap)
     lanes = -(-half_cap // 128) * 128
     gate_rows = jnp.broadcast_to(
         jnp.pad(gate_rows, ((0, 0), (0, lanes - half_cap)))[:, None, :], (experts, 8, lanes)
     )
 
-    got_rows, got_gates = exchange(
-        "dispatch", 3, sizes,
-        [
-            Item(
-                "all", sent_rows, [shape_of((tps, groups, half_cap, width), BF16)],
-                lambda ref, p: ref.at[p],
-                lambda ref, q, t: ref.at[0, q],
-                relay=lambda ref, q, t: ref.at[1, q],
-                block=(half_cap, width),
-            ),
-            Item(
-                "all", gate_rows, [shape_of((tps, groups, 8, lanes), F32)],
-                lambda ref, p: ref.at[p],
-                lambda ref, q, t: ref.at[0, q],
-                relay=lambda ref, q, t: ref.at[1, q],
-                block=(8, lanes),
-            ),
-        ],
-    )
-
-    total_rows = tps * groups * half_cap
+    def scattered(array):
+        block = array.shape[1:]
+        return Item(
+            "all", array, [shape_of((tps,) + array.shape, array.dtype)],
+            lambda ref, p: ref.at[p],
+            lambda ref, q, t: ref.at[0, q],
+            relay=lambda ref, q, t: ref.at[1, q],
+            block=block,
+        )
+
+    got_gates, got_rows, cot_par = exchange(
+        "dispatch", 3, sizes, [scattered(gate_rows), scattered(sent_rows), passed(got_cot)]
+    )
+
+    slots_half = groups * half_cap
+    total_rows = tps * slots_half
     arrived = got_rows.reshape(total_rows, width)
     gates = got_gates[:, :, 0, :half_cap].reshape(total_rows)
     cot_rows = jnp.concatenate([got_cot, cot_par], axis=0).reshape(total_rows, width)
@@ -564,62 +843,26 @@
     hidden, gelu_back = jax.vjp(jax.nn.gelu, pre)
     hidden = hidden.astype(BF16)
     partial_out = nn(hidden, w_out[0]).astype(BF16).reshape(tps, groups, half_cap, width)
-
-    def pair_item(array, index):
-        return Item(
-            "pair", array, [shape_of(array.shape[1:], BF16)],
-            lambda ref, p: ref.at[index], None, relay=lambda ref, q, t: ref, keep=False,
-        )
-
-    (out_par,) = exchange("sum_out", 4, sizes, [pair_item(partial_out, 1)])
-    summed = (partial_out[0].astype(F32) + out_par.astype(F32)).astype(BF16)
+    summed = pair_sum("sum_out", 4, partial_out)
     going_back = lax.all_to_all(summed, group, split_axis=0, concat_axis=0, tiled=True)
 
-    grad_w_out = tn(hidden, grad_rows)[None]
     grad_hidden = nt(grad_rows, w_out[0])
     grad_pre = gelu_back(grad_hidden)[0].astype(BF16)
     partial_grad = nt(grad_pre, w_in[0]).astype(BF16).reshape(tps, groups, half_cap, width)
-    grad_w_in = tn(arrived, grad_pre)[None]
-
-    (grad_par,) = exchange("sum_grad", 5, sizes, [pair_item(partial_grad, 1)])
-    grad_summed = (partial_grad[0].astype(F32) + grad_par.astype(F32)).astype(BF16)
+    grad_summed = pair_sum("sum_grad", 5, partial_grad)
     grad_home, back_par = exchange(
-        "grad_home", 6, sizes,
-        [
-            Item(
-                "all", grad_summed, [shape_of((tps, groups, half_cap, width), BF16)],
-                lambda ref, p: ref.at[p],
-                lambda ref, q, t: ref.at[0, q],
-                relay=lambda ref, q, t: ref.at[1, q],
-                block=(half_cap, width),
-            ),
-            Item(
-                "pair", going_back, [shape_of(going_back.shape, BF16)],
-                lambda ref, p: ref, None, relay=lambda ref, q, t: ref, keep=False,
-            ),
-        ],
-    )
-
-    slots_half = experts * half_cap
-    fetched = tn(pick_own, going_back.reshape(slots_half, width)) + tn(
-        pick_par, back_par.reshape(slots_half, width)
-    )
-    grad_home = grad_home.reshape(tps, slots_half, width)
-    grad_home_rows = tn(pick_own, grad_home[0]) + tn(pick_par, grad_home[1])
-    kept_value = kept.astype(F32)
-    valid_value = valid.astype(F32)
-    output = (
-        (valid_value[:, None] * (middle + (kept_value * gate)[:, None] * fetched))
-        .astype(BF16)
-        .reshape(slots, count, width)
-    )
-    grad_out = valid_value[:, None] * cot.astype(F32)
-    grad_gate = kept_value * jnp.sum(grad_out * fetched, axis=1)
-    grad_logits = ((grad_gate * gate)[:, None] * (route_hot.astype(F32) - probs)).astype(BF16)
-    grad_second = grad_home_rows + nt(grad_logits, full_router)
-    grad_middle = grad_out + norm_back(grad_second * full_two, unit_two, inverse_two)
-    grad_branch = grad_middle.astype(BF16)
-    grad_mixed_own = nn(grad_branch, whole_proj).astype(BF16)
+        "grad_home", 6, sizes, [scattered(grad_summed), passed(going_back)]
+    )
+
+    where = jnp.stack([ctx_rank * count, lengths[0]]).astype(jnp.int32)
+    output, grad_middle, grad_branch, grad_mixed_own, grad_logits, grad_gain_two = home_step(
+        cot, middle, second, probs, gate, route_column, target.reshape(count, 1),
+        own_slot.reshape(1, slots_half), par_slot.reshape(1, slots_half),
+        going_back.reshape(slots_half, width), back_par.reshape(slots_half, width),
+        grad_home.reshape(tps, slots_half, width), full_two, full_small, whole_proj, where, experts,
+        experts * capacity,
+    )
+    output = output.reshape(slots, count, width)
 
     (grad_mixed,) = exchange(
         "grad_mixed", 7, sizes,
@@ -632,11 +875,13 @@
             ),
         ],
     )
-    grad_router = tn(second, grad_logits)
-    grad_gain_two = jnp.sum(grad_second * unit_two, axis=0)
+    grad_router = tn(second, grad_logits)[:, :experts]
     grad_proj = tn(grad_branch, mixed_own)
     packed = jnp.concatenate(
-        [grad_proj, grad_router, grad_gain_two[:, None], jnp.zeros((width, pad - experts - 1), F32)],
+        [
+            grad_proj, grad_router, grad_gain_two.reshape(width, 1),
+            jnp.zeros((width, pad - experts - 1), F32),
+        ],
         axis=1,
     )
     owned = lax.psum_scatter(packed, group, scatter_dimension=0, tiled=True)
@@ -645,38 +890,23 @@
     owned_two = owned[:, head_width + experts]
 
     grad_projected = attention_backward(projected, mixed_heads, grad_mixed, lse, lengths, heads)
-    grad_weight = tn(unit_all, grad_projected).astype(BF16).reshape(groups, rows, 3 * wide)
-    grad_own, grad_par, got_grad = exchange(
-        "grad_projected", 8, sizes,
-        [
-            Item(
-                "ctx", grad_projected,
-                [shape_of((count, 3 * head_width), BF16), shape_of((count, 3 * head_width), BF16)],
-                lambda ref, p: ref.at[pl.ds(pl.multiple_of(p * count, count), count), :],
-                lambda ref, q, t: ref.at[:, pl.ds(pl.multiple_of(q * 3 * wide, wide), 3 * wide)],
-                relay=lambda ref, q, t: ref.at[:, pl.ds(pl.multiple_of(q * 3 * wide, wide), 3 * wide)],
-                block=(count, 3 * wide),
-            ),
-            Item(
-                "all", grad_weight, [shape_of((groups, rows, 3 * wide), BF16)],
-                lambda ref, p: ref.at[p],
-                lambda ref, q, t: ref.at[q],
-                block=(rows, 3 * wide),
-            ),
-        ],
-    )
-    scaled_first = nt(grad_own, whole_qkv) + nt(grad_par, qkv_par)
-    unit_one, inverse_one = normed(inputs)
-    grad_tokens = (grad_middle + norm_back(scaled_first, unit_one, inverse_one)).reshape(
-        slots, count, width
-    )
-    raw = (
-        jnp.sum(got_grad.astype(F32).reshape(shards, ctxs, rows, 3, wide), axis=0)
-        .transpose(2, 1, 0, 3)
-        .reshape(3, rows, head_width)
-    )
-    owned_qkv = raw * gain_one.astype(F32)[None, :, None]
-    owned_one = lax.psum(jnp.sum(raw * weight_qkv.astype(F32), axis=(0, 2)), "tp")
+    grad_own = lax.all_to_all(
+        grad_projected.reshape(ctxs, count, 3 * wide), "ctx", split_axis=0, concat_axis=0, tiled=True
+    )
+
+    unit_late, hidden, arrived, grad_rows, grad_pre, grad_projected = lax.optimization_barrier(
+        (unit_all, hidden, arrived, grad_rows, grad_pre, grad_projected)
+    )
+    grad_weight = tn(unit_late, grad_projected).astype(BF16).reshape(groups, rows, 3 * wide)
+    got_grad = lax.all_to_all(grad_weight, group, split_axis=0, concat_axis=0, tiled=True)
+    grad_w_out = tn(hidden, grad_rows)[None]
+    grad_w_in = tn(arrived, grad_pre)[None]
+
+    (grad_par,) = exchange("grad_pair", 8, sizes, [passed(grad_own)])
+    grad_tokens = last_step(rows_in, grad_middle, grad_own, grad_par, whole_qkv, qkv_par)
+    grad_tokens = grad_tokens.reshape(slots, count, width)
+    owned_qkv, sums = owner_step(got_grad, weight_qkv, gain_one.reshape(rows, 1), shards, ctxs, wide)
+    owned_one = lax.psum(sums[:, 0], "tp")
     return (
         output,
         grad_tokens,

time: 600 us -> 632 us (1.053); the launches traced: 590 us -> 630 us
  waiting for transfers between devices: 7.98 us -> 111 us
  blocking collectives: 3 us -> 62.2 us
  Pallas kernels: 354 us -> 295 us
  local copies, waits for them, and re-layouts: 46.3 us -> 18.6 us
  matrix products: 118 us -> 94.2 us
  other arithmetic: 32.4 us -> 10.2 us
  starting transfers between devices: 13 us -> 23.1 us
    pallas_call x8 -> x6, Pallas kernels: 277 us -> 165 us  [exchange(): pl.pallas_call(body, name=name, out_shape=tuple(out_shapes), in_specs=[an...]
    all_gather x2, waiting for transfers between devices: 0.02 us -> 79 us  [the longest x1 70.1 us: local(): whole_qkv = lax.all_gather(row_weights, group, axis=0, tiled=True)]
    all_to_all x0 -> x1, blocking collectives: none -> 59.2 us  [local(): lax.all_to_all(grad_weight, group, split_axis=0, concat_axis=0, tiled=True)]
    pallas_call x1 -> x8, Pallas kernels: 35.1 us -> 87.2 us  [the longest x1 30.7 us: attention_forward(): pl.pallas_call(functools.partial(forward_kernel, heads, size, span, count...]
    all_to_all x0 -> x1, waiting for transfers between devices: none -> 31.6 us  [local(): lax.all_to_all(grad_projected.reshape(ctxs, count, 3 * wide), 'ctx', spli...]
    unnamed x91 -> x42, local copies, waits for them, and re-layouts: 23.8 us -> 8.23 us
    dot_general x7 -> x2, matrix products: 37.7 us -> 25.3 us  [nt(): lax.dot_general(left, right, (((1,), (1,)), ((), ())), preferred_element_...]
    convert_element_type x8 -> x1, other arithmetic: 12.2 us -> 0.01 us  [local(): place = jnp.sum(earlier * counted.astype(F32), axis=1).astype(jnp.int32)]
  transfers between devices with their start and end apart: 5 -> 6, of which waited for: 1 -> 3; matrix products, arithmetic and copies ran while one was open for 16% -> 14% of each run, Pallas kernels for 39% -> 13%
where the time goes in v2:
time: 632 us; the launch traced here: 630 us
  Pallas kernels  295 us (47%)
  waiting for transfers between devices  111 us (18%)
  matrix products  94.2 us (15%)
  blocking collectives  62.2 us (10%)
  starting transfers between devices  23.1 us (4%)
  local copies, waits for them, and re-layouts  18.6 us (3%)
  between operations  15 us (2%)
  other arithmetic  10.2 us (2%)
    pallas_call x6, Pallas kernels, exchange(): pl.pallas_call(body, name=name, out_shape=tuple(out_shapes), in_specs=[an...  165 us
    all_gather x1, waiting for transfers between devices, local(): whole_qkv = lax.all_gather(row_weights, group, axis=0, tiled=True)  70.1 us
    all_to_all x1, blocking collectives, local(): lax.all_to_all(grad_weight, group, split_axis=0, concat_axis=0, tiled=True)  59.2 us
    pallas_call x1, Pallas kernels, attention_backward(): pl.pallas_call(functools.partial(backward_kernel, heads, size, blocks), n...  42.7 us
    dot_general x6, matrix products, nn(): lax.dot_general(left, right, (((1,), (0,)), ((), ())), preferred_element_...  37 us
    dot_general x5, matrix products, tn(): lax.dot_general(left, right, (((0,), (0,)), ((), ())), preferred_element_...  31.9 us
    all_to_all x1, waiting for transfers between devices, local(): lax.all_to_all(grad_projected.reshape(ctxs, count, 3 * wide), 'ctx', spli...  31.6 us
    pallas_call x1, Pallas kernels, attention_forward(): pl.pallas_call(functools.partial(forward_kernel, heads, size, span, count...  30.7 us
  transfers between devices with their start and end apart: 6, of which 3 were waited for; matrix products, arithmetic and copies ran while one was open for 14% of the time, Pallas kernels for 13%

profile of v2, /device:TPU:0, one launch (start us, length us, event | category | flops | bytes accessed | tf_op | source)
XLA Modules:
  0.0 630.0 jit_solution(16181640088723645873)
XLA Ops:
  10.5 3.1 prepare.1
  13.6 67.3 %gather_rows.1 = (bf16[4,2,512,1024]{3,2,1,0:T(8,128)(2,1)}, bf16[16,64,512]{2,1,0:T(8,128)(2,1)}) custom-call(bf16[512,1024]{1,0:T(8,128)(2,1)} %get-tuple-element.49.refs_0_, bf16[4,64,512]{2,1,0:T(8,128)(2,1)} %get-tuple-element.50.refs_1_), custom_call_target="tpu_custom_call" | custom-call | tf_op jit(solution)/shard_map/gather_rows/pallas_call | solution.py:174
  83.6 2.6 fusion.33
  86.3 3.9 all-to-all-start
  95.2 9.1 %convolution_convert_fusion.q_ref.k_ref.v_ref = bf16[4096,384]{1,0:T(8,128)(2,1)} fusion(bf16[4096,1024]{1,0:T(8,128)(2,1)} %bitcast.101, bf16[1024,512]{1,0:T(8,128)(2,1)S(1)} %bitcast.91), kind=kOutput, calls=%fused_computation.10 | convolution fusion | flops 3222798336 | bytes 12320768 | tf_op jit(solution)/shard_map/dot_general | solution.py:190
  104.3 30.7 %attention_forward.1 = (bf16[4096,128]{1,0:T(8,128)(2,1)}, f32[8,1,1024]{2,1,0:T(1,128)}) custom-call(s32[1]{0:T(128)} %copy.60.len_ref, bf16[4096,384]{1,0:T(8,128)(2,1)} %convolution_convert_fusion.q_ref.k_ref.v_ref, bf16[4096,384]{1,0:T(8,128)(2,1)} %convolution_convert_fusion.q_ref.k_ref.v_ref, bf16[4096,384]{1,0:T(8,128)(2,1)} %convolution_convert_fusion.q_ref.k_ref.v_ref), custom_call_target="tpu_custom_call" | custom-call | flops 34359738368 | bytes 4194304 | tf_op jit(solution)/shard_map/attention_forward/pallas_call | solution.py:264
  134.9 8.9 %all-gather.3.cloned.1.call-done.refs_1_.proj_own_ref.proj_ref = bf16[1024,512]{1,0:T(8,128)(2,1)} async-done(((bf16[64,512]{1,0:T(8,128)(2,1)}), bf16[1024,512]{1,0:T(8,128)(2,1)}) %all-gather.3.cloned.1.call-update) | async-done | bytes 1048592 | tf_op jit(solution)/shard_map/all_gather | solution.py:757
  143.8 70.1 %all-gather.5.cloned.1.call-done.refs_2_.weight_own_ref = bf16[1024,1536]{1,0:T(8,128)(2,1)} async-done(((bf16[64,1536]{1,0:T(8,128)(2,1)}), bf16[1024,1536]{1,0:T(8,128)(2,1)}) %all-gather.5.cloned.1.call-update) | async-done | bytes 3145744 | tf_op jit(solution)/shard_map/all_gather | solution.py:756
  213.9 16.5 %mixed_home.1 = (bf16[1024,512]{1,0:T(8,128)(2,1)}, bf16[1024,512]{1,0:T(8,128)(2,1)}, bf16[1024,512]{1,0:T(8,128)(2,1)}, bf16[1024,1536]{1,0:T(8,128)(2,1)}) custom-call(bf16[4096,128]{1,0:T(8,128)(2,1)} %get-tuple-element.56.refs_0_.o_ref, bf16[1024,512]{1,0:T(8,128)(2,1)} %all-gather.3.cloned.1.call-done.refs_1_.proj_own_ref.proj_ref, ...), custom_call_target="tpu_custom_call" | custom-call | tf_op jit(solution)/shard_map/mixed_home/pallas_call | solution.py:174
  230.4 8.9 %middle_step.1 = (f32[1024,1024]{1,0:T(8,128)}, bf16[1024,1024]{1,0:T(8,128)(2,1)}, f32[1024,128]{1,0:T(8,128)}, f32[1024,1]{1,0:T(8,128)}) custom-call(bf16[1024,1024]{1,0:T(8,128)(2,1)} %bitcast.75, bf16[1024,512]{1,0:T(8,128)(2,1)} %get-tuple-element.59.own_ref, bf16[1024,512]{1,0:T(8,128)(2,1)} %get-tuple-element.60.par_ref, ...), custom_call_target="tpu_custom_call" | custom-call | tf_op jit(solution)/shard_map/middle_step/pallas_call | solution.py:541
  241.1 4.2 fusion.30
  246.4 28.0 %dispatch.1 = (f32[2,16,8,128]{3,2,1,0:T(8,128)}, bf16[2,16,40,1024]{3,2,1,0:T(8,128)(2,1)}, bf16[16,40,1024]{2,1,0:T(8,128)(2,1)}) custom-call(f32[16,8,128]{2,1,0:T(8,128)} %broadcast_in_dim.62.refs_0_, bf16[16,40,1024]{2,1,0:T(8,128)(2,1)} %bitcast.87, bf16[16,40,1024]{2,1,0:T(8,128)(2,1)} %copy-done.1), custom_call_target="tpu_custom_call" | custom-call | tf_op jit(solution)/shard_map/dispatch/pallas_call | solution.py:174
  275.4 12.9 %multiply_convert_fusion = (bf16[1280,2048]{1,0:T(8,128)(2,1)S(1)}, f32[1280,2048]{1,0:T(8,128)}) fusion(bf16[1280,1024]{1,0:T(8,128)(2,1)} %bitcast.103, bf16[1,1024,2048]{2,1,0:T(8,128)(2,1)} %param.19), kind=kOutput, calls=%fused_computation.9 | convolution fusion | flops 5392302080 | bytes 22544384 | tf_op jit(solution)/shard_map/dot_general | solution.py:190
  288.3 6.9 %fusion.26 = bf16[1280,1024]{1,0:T(8,128)(2,1)} fusion(bf16[1280,2048]{1,0:T(8,128)(2,1)S(1)} %get-tuple-element.87, bf16[1,2048,1024]{2,1,0:T(8,128)(2,1)S(1)} %copy-done.14), kind=kOutput, calls=%fused_computation.32 | convolution fusion | flops 5370019840 | bytes 12058624 | tf_op jit(solution)/shard_map/dot_general | solution.py:190
  295.2 4.8 sum_out.1
  300.0 15.2 %all-to-all-start.1 = ((bf16[16,40,1024]{2,1,0:T(8,128)(2,1)}), bf16[16,40,1024]{2,1,0:T(8,128)(2,1)S(1)}, u32[]{:S(2)}, u32[]{:S(2)}) async-start(bf16[16,40,1024]{2,1,0:T(8,128)(2,1)} %sum_out.1), calls=%async_computation.1 | async-start | bytes 2621440 | tf_op jit(solution)/shard_map/all_to_all | solution.py:847
  317.8 15.2 %fusion.6 = bf16[1280,2048]{1,0:T(8,128)(2,1)} fusion(f32[1280,2048]{1,0:T(8,128)} %get-tuple-element.128, bf16[1280,1024]{1,0:T(8,128)(2,1)S(1)} %bitcast.81, bf16[1,2048,1024]{2,1,0:T(8,128)(2,1)S(1)} %copy-done.15), kind=kOutput, calls=%fused_computation.8 | convolution fusion | flops 5421137920 | bytes 22544384 | tf_op jit(solution)/shard_map/dot_general | solution.py:186
  333.1 10.2 %fusion.23 = bf16[1280,1024]{1,0:T(8,128)(2,1)} fusion(bf16[1280,2048]{1,0:T(8,128)(2,1)} %fusion.6, bf16[1,1024,2048]{2,1,0:T(8,128)(2,1)} %param.19), kind=kOutput, calls=%fused_computation.31 | convolution fusion | flops 5370019840 | bytes 12058624 | tf_op jit(solution)/shard_map/dot_general | solution.py:186
  343.2 4.7 sum_grad.1.refs_0_
  352.5 28.0 %grad_home.1 = (bf16[2,16,40,1024]{3,2,1,0:T(8,128)(2,1)}, bf16[16,40,1024]{2,1,0:T(8,128)(2,1)}) custom-call(bf16[16,40,1024]{2,1,0:T(8,128)(2,1)} %sum_grad.1.refs_0_, bf16[16,40,1024]{2,1,0:T(8,128)(2,1)} %copy-done.3), custom_call_target="tpu_custom_call" | custom-call | tf_op jit(solution)/shard_map/grad_home/pallas_call | solution.py:174
  380.5 17.6 %home_step.1 = (bf16[1024,1024]{1,0:T(8,128)(2,1)}, f32[1024,1024]{1,0:T(8,128)}, bf16[1024,1024]{1,0:T(8,128)(2,1)}, bf16[1024,512]{1,0:T(8,128)(2,1)}, bf16[1024,128]{1,0:T(8,128)(2,1)}, /*index=5*/f32[1,1024]{1,0:T(1,128)}) custom-call(s32[2]{0:T(128)} %pad_add_fusion.where_ref, bf16[1024,1024]{1,0:T(8,128)(2,1)} %bitcast.84, ...), custom_call_target="tpu_custom_call" | custom-call | tf_op jit(solution)/shard_map/home_step/pallas_call | solution.py:619
  398.1 19.6 %grad_mixed.1.do_ref = bf16[4096,128]{1,0:T(8,128)(2,1)} custom-call(bf16[1024,512]{1,0:T(8,128)(2,1)} %get-tuple-element.75.refs_0_), custom_call_target="tpu_custom_call" | custom-call | tf_op jit(solution)/shard_map/grad_mixed/pallas_call | solution.py:174
  417.7 42.7 %attention_backward.1 = bf16[4096,384]{1,0:T(8,128)(2,1)} custom-call(s32[1]{0:T(128)} %copy.60.len_ref, bf16[4096,384]{1,0:T(8,128)(2,1)} %convolution_convert_fusion.q_ref.k_ref.v_ref, bf16[4096,384]{1,0:T(8,128)(2,1)} %convolution_convert_fusion.q_ref.k_ref.v_ref, bf16[4096,384]{1,0:T(8,128)(2,1)} %convolution_convert_fusion.q_ref.k_ref.v_ref, ...), custom_call_target="tpu_custom_call" | custom-call | flops 85899345920 | bytes 8388608 | tf_op jit(solution)/shard_map/attention_backward/pallas_call | solution.py:373
  464.8 8.8 %convolution_convert_fusion.1 = bf16[1024,384]{1,0:T(8,128)(2,1)S(1)} fusion(bf16[4096,1024]{1,0:T(8,128)(2,1)} %bitcast.102, bf16[4096,384]{1,0:T(8,128)(2,1)} %attention_backward.1), kind=kOutput, calls=%fused_computation.38 | convolution fusion | flops 3221618688 | bytes 12320768 | tf_op jit(solution)/shard_map/dot_general | solution.py:194
  473.6 59.2 %all_to_all.20.got_ref = bf16[16,64,384]{2,1,0:T(8,128)(2,1)} all-to-all(bf16[16,64,384]{2,1,0:T(8,128)(2,1)S(1)} %bitcast.88), channel_id=1, replica_groups=mesh['shard'=4,'ctx'=4,'tp'=2] {'shard','ctx'}, dimensions={0} | all-to-all | bytes 1572864 | tf_op jit(solution)/shard_map/all_to_all | solution.py:901
  532.8 3.9 all-to-all-start.2
  536.7 11.0 %convolution_bitcast_fusion = f32[1,2048,1024]{2,1,0:T(8,128)} fusion(bf16[1280,2048]{1,0:T(8,128)(2,1)} %copy-done.18, bf16[1280,1024]{1,0:T(8,128)(2,1)} %fusion.7), kind=kOutput, calls=%fused_computation.14 | convolution fusion | flops 5368709120 | bytes 16252928 | tf_op jit(solution)/shard_map/dot_general | solution.py:194
  547.7 10.4 %convolution_bitcast_fusion.1 = f32[1,1024,2048]{2,1,0:T(8,128)} fusion(bf16[1280,1024]{1,0:T(8,128)(2,1)S(1)} %bitcast.104, bf16[1280,2048]{1,0:T(8,128)(2,1)} %fusion.6), kind=kOutput, calls=%fused_computation.15 | convolution fusion | flops 5368709120 | bytes 16252928 | tf_op jit(solution)/shard_map/dot_general | solution.py:194
  561.2 3.0 psum.7
  564.1 31.6 %all-to-all-done.2.refs_0_.own_ref = bf16[4,1024,384]{2,1,0:T(8,128)(2,1)S(1)} async-done(((bf16[4,1024,384]{2,1,0:T(8,128)(2,1)}), bf16[4,1024,384]{2,1,0:T(8,128)(2,1)S(1)}, u32[]{:S(2)}, u32[]{:S(2)}) %all-to-all-start.2) | async-done | bytes 3145760 | tf_op jit(solution)/shard_map/all_to_all | solution.py:893
  597.4 6.1 grad_pair.1.par_ref
  603.5 15.3 %last_step.1 = f32[1024,1024]{1,0:T(8,128)} custom-call(bf16[1024,1024]{1,0:T(8,128)(2,1)} %bitcast.76, f32[1024,1024]{1,0:T(8,128)} %get-tuple-element.74.grad_middle_ref, bf16[4,1024,384]{2,1,0:T(8,128)(2,1)} %copy-done, bf16[4,1024,384]{2,1,0:T(8,128)(2,1)} %grad_pair.1.par_ref, bf16[1024,1536]{1,0:T(8,128)(2,1)} %all-gather.5.cloned.1.call-done.refs_2_.weight_own_ref, ...), custom_call_target="tpu_custom_call" | custom-call | tf_op jit(solution)/shard_map/last_step/pallas_call | solution.py:667
  (89 shorter events, 34.8 us)
Async XLA Ops:
  7.2 76.4 %copy-start.6 = (bf16[1,1024,1024]{2,1,0:T(8,128)(2,1)S(1)}, bf16[1,1024,1024]{2,1,0:T(8,128)(2,1)}, u32[]{:S(2)}) copy-start(bf16[1,1024,1024]{2,1,0:T(8,128)(2,1)} %param.21) | copy-start | bytes 6291460
  7.2 76.4 %copy-start.12 = (s32[1,1024,1]{1,2,0:T(1,128)S(1)}, s32[1,1024,1]{1,2,0:T(1,128)}, u32[]{:S(2)}) copy-start(s32[1,1024,1]{1,2,0:T(1,128)} %param.13) | copy-start | bytes 12292
  7.2 136.6 %all-gather.3.cloned.1.call-start = ((), (), s32[]{:S(2)}) async-start(), calls=%async_computation.5 | async-start | bytes 1114112 | tf_op jit(solution)/shard_map/all_gather | solution.py:757
  8.1 78.1 %copy-start.10 = (bf16[64,1]{1,0:T(8,128)(2,1)}, bf16[64,1]{1,0:T(8,128)(2,1)S(1)}, u32[]{:S(2)}) copy-start(bf16[64,1]{1,0:T(8,128)(2,1)S(1)} %copy.47.gain_ref) | copy-start | bytes 388
  80.9 133.0 %all-gather.5.cloned.1.call-start = ((), (), s32[]{:S(2)}) async-start(), calls=%async_computation.6 | async-start | bytes 3342336 | tf_op jit(solution)/shard_map/all_gather | solution.py:756
  83.6 6.8 %copy-start.9 = (bf16[16,64,512]{2,1,0:T(8,128)(2,1)S(1)}, bf16[16,64,512]{2,1,0:T(8,128)(2,1)}, u32[]{:S(2)}) copy-start(bf16[16,64,512]{2,1,0:T(8,128)(2,1)} %get-tuple-element.55) | copy-start | bytes 3145732
  86.3 159.1 %all-to-all-start = ((bf16[16,40,1024]{2,1,0:T(8,128)(2,1)}), bf16[16,40,1024]{2,1,0:T(8,128)(2,1)S(1)}, u32[]{:S(2)}, u32[]{:S(2)}) async-start(bf16[16,40,1024]{2,1,0:T(8,128)(2,1)} %bitcast.13), calls=%async_computation | async-start | bytes 2621440 | tf_op jit(solution)/shard_map/all_to_all | solution.py:783
  90.4 13.8 %copy-start.5 = (s32[1024,1]{1,0:T(8,128)}, s32[1024,1]{1,0:T(8,128)S(1)}, u32[]{:S(2)}) copy-start(s32[1024,1]{1,0:T(8,128)S(1)} %copy.48.route_ref) | copy-start | bytes 12292
  245.3 1.1 copy-start.1
  275.4 13.0 %copy-start.14 = (bf16[1,2048,1024]{2,1,0:T(8,128)(2,1)S(1)}, bf16[1,2048,1024]{2,1,0:T(8,128)(2,1)}, u32[]{:S(2)}) copy-start(bf16[1,2048,1024]{2,1,0:T(8,128)(2,1)} %param.20) | copy-start | bytes 12582916
  288.3 6.9 %copy-start.18 = (bf16[1280,2048]{1,0:T(8,128)(2,1)}, bf16[1280,2048]{1,0:T(8,128)(2,1)S(1)}, u32[]{:S(2)}) copy-start(bf16[1280,2048]{1,0:T(8,128)(2,1)S(1)} %get-tuple-element.87) | copy-start | bytes 15728644
  295.2 20.1 %copy-start.2 = (bf16[16,40,1024]{2,1,0:T(8,128)(2,1)S(1)}, bf16[16,40,1024]{2,1,0:T(8,128)(2,1)}, u32[]{:S(2)}) copy-start(bf16[16,40,1024]{2,1,0:T(8,128)(2,1)} %copy-done.1) | copy-start | bytes 3932164
  300.0 51.5 %all-to-all-start.1 = ((bf16[16,40,1024]{2,1,0:T(8,128)(2,1)}), bf16[16,40,1024]{2,1,0:T(8,128)(2,1)S(1)}, u32[]{:S(2)}, u32[]{:S(2)}) async-start(bf16[16,40,1024]{2,1,0:T(8,128)(2,1)} %sum_out.1), calls=%async_computation.1 | async-start | bytes 2621440 | tf_op jit(solution)/shard_map/all_to_all | solution.py:847
  315.2 303.6 %reduce-scatter.4.cloned.1.call-start = ((), (), s32[]{:S(2)}) async-start(), calls=%async_computation.7 | async-start | bytes 2785280
  315.2 2.6 copy-start.15
  351.5 1.1 copy-start.3
  417.7 42.7 %copy-start.7 = (bf16[1024,512]{1,0:T(8,128)(2,1)S(1)}, bf16[1024,512]{1,0:T(8,128)(2,1)}, u32[]{:S(2)}) copy-start(bf16[1024,512]{1,0:T(8,128)(2,1)} %get-tuple-element.59.own_ref) | copy-start | bytes 3145732
  417.7 42.7 %copy-start.17 = (bf16[1024,1024]{1,0:T(8,128)(2,1)S(1)}, bf16[1024,1024]{1,0:T(8,128)(2,1)}, u32[]{:S(2)}) copy-start(bf16[1024,1024]{1,0:T(8,128)(2,1)} %get-tuple-element.81) | copy-start | bytes 6291460
  460.4 1.6 copy-start.4
  460.4 1.6 copy-start.8
  460.4 2.0 copy-start.11
  460.4 2.0 copy-start.13
  532.8 62.9 %all-to-all-start.2 = ((bf16[4,1024,384]{2,1,0:T(8,128)(2,1)}), bf16[4,1024,384]{2,1,0:T(8,128)(2,1)S(1)}, u32[]{:S(2)}, u32[]{:S(2)}) async-start(bf16[4,1024,384]{2,1,0:T(8,128)(2,1)} %bitcast.79), calls=%async_computation.2 | async-start | bytes 6291456 | tf_op jit(solution)/shard_map/all_to_all | solution.py:893
  536.7 11.0 %copy-start.16 = (bf16[2,16,40,1024]{3,2,1,0:T(8,128)(2,1)S(1)}, bf16[2,16,40,1024]{3,2,1,0:T(8,128)(2,1)}, u32[]{:S(2)}) copy-start(bf16[2,16,40,1024]{3,2,1,0:T(8,128)(2,1)} %get-tuple-element.68) | copy-start | bytes 7864324
  595.7 1.7 copy-start
Sparse Core Ops, SparseCore 0:
  81.0 62.7 all-gather.2
  147.2 66.6 all-gather.4
  464.9 124.0 reduce-scatter.3

commit v3 on v2

--- a/solution.py
+++ b/solution.py
@@ -12,6 +12,8 @@
 MASKED = -1e30
 LOG2E = 1.4426950408889634
 BLOCK = 512
+GELU_A = 0.7978845608028654
+GELU_B = 0.044715
 MESH = pl.DeviceIdType.MESH
 BF16 = jnp.bfloat16
 F32 = jnp.float32
@@ -23,7 +25,7 @@
         self.src, self.dst, self.relay, self.block, self.keep = src, dst, relay, block, keep
 
 
-def exchange(name, collective_id, sizes, items):
+def exchange(collective_id, sizes, items):
     shards, ctxs, tps = sizes
     count_all = shards * ctxs
     operands = [item.ins for item in items]
@@ -83,7 +85,6 @@
             jobs.append((item, source, outs, sems, stage))
 
         def make(item, source, outs, sems, k, peer, sender):
-            mine = {"ctx": me_c, "all": me_all}[item.group]
             return pltpu.make_async_remote_copy(
                 src_ref=item.src(source, peer),
                 dst_ref=item.dst(outs[0], sender, me_t),
@@ -173,13 +174,164 @@
     anywhere = pl.BlockSpec(memory_space=pl.ANY)
     return pl.pallas_call(
         body,
-        name=name,
         out_shape=tuple(out_shapes),
         in_specs=[anywhere] * len(operands),
         out_specs=tuple([anywhere] * len(out_shapes)),
         scratch_shapes=scratch,
         compiler_params=pltpu.CompilerParams(collective_id=collective_id, has_side_effects=True),
     )(*operands)
+
+
+def gather_step(collective_id, sizes, unit_half, weights):
+    shards, ctxs, tps = sizes
+    groups = shards * ctxs
+    assert ctxs == 4 and tps == 2
+    half, width = unit_half.shape
+    part = half // 2
+    piece = weights.shape[1:]
+
+    def body(rows_ref, weights_ref, all_ref, got_ref, rows_stage, weights_stage, send, take, relay, taken, put, away, home):
+        me_s, me_c, me_t = lax.axis_index("shard"), lax.axis_index("ctx"), lax.axis_index("tp")
+        me = me_s * ctxs + me_c
+        low = me_c % 2
+        high = me_c // 2
+        near = high * 2 + (1 - low)
+        side = (1 - high) * 2 + low
+        far = (1 - high) * 2 + (1 - low)
+        partner = {"tp": 1 - me_t}
+
+        def place(p):
+            return {"shard": p // ctxs, "ctx": p % ctxs}
+
+        barrier = pltpu.get_barrier_semaphore()
+
+        def greet(k, carry):
+            pl.semaphore_signal(
+                barrier, inc=1, device_id=place(lax.rem(me + k, groups)), device_id_type=MESH
+            )
+            return carry
+
+        lax.fori_loop(1, groups, greet, 0)
+        pl.semaphore_signal(barrier, inc=1, device_id=partner, device_id_type=MESH)
+        pl.semaphore_wait(barrier, groups)
+
+        def copy(src, dst, src_sem, dst_sem, device):
+            return pltpu.make_async_remote_copy(
+                src_ref=src, dst_ref=dst, send_sem=src_sem, recv_sem=dst_sem,
+                device_id=device, device_id_type=MESH,
+            )
+
+        def rows_of(p):
+            return rows_ref.at[pl.ds(p * part, part), :]
+
+        def slot(q, p):
+            return all_ref.at[q, me_t, pl.ds(p * part, part), :]
+
+        to_near = [copy(rows_of(p), slot(me_c, p), send.at[p], take.at[p], {"ctx": near}) for p in (0, 1)]
+        to_side = [
+            copy(rows_of(1 - p), slot(me_c, 1 - p), send.at[2 + p], take.at[2 + p], {"ctx": side})
+            for p in (0, 1)
+        ]
+        for p in (0, 1):
+            to_near[p].start()
+            to_side[p].start()
+        mine = copy(rows_ref, all_ref.at[me_c, me_t], relay.at[6], taken.at[6], partner)
+        mine.start()
+
+        def weights_to(k, carry):
+            peer = lax.rem(me + k, groups)
+            copy(
+                weights_ref.at[peer % ctxs], got_ref.at[me], put.at[k], away.at[me], place(peer)
+            ).start()
+            return carry
+
+        lax.fori_loop(1, groups, weights_to, 0)
+        stays = [
+            pltpu.make_async_copy(rows_ref, rows_stage, home.at[0]),
+            pltpu.make_async_copy(weights_ref.at[me_c], weights_stage, home.at[1]),
+        ]
+        lands = [
+            pltpu.make_async_copy(rows_stage, all_ref.at[me_c, me_t], home.at[2]),
+            pltpu.make_async_copy(weights_stage, got_ref.at[me], home.at[3]),
+        ]
+        for stay in stays:
+            stay.start()
+        for stay, land in zip(stays, lands):
+            stay.wait()
+            land.start()
+
+        got = [slot(near, 0), slot(near, 1), slot(side, 1), slot(side, 0), slot(far, 0), slot(far, 1)]
+        relays = [copy(ref, ref, relay.at[n], taken.at[n], partner) for n, ref in enumerate(got)]
+        on_side = copy(got[0], got[0], send.at[4], take.at[4], {"ctx": side})
+        on_near = copy(got[2], got[2], send.at[5], take.at[5], {"ctx": near})
+        to_near[0].wait_recv()
+        on_side.start()
+        relays[0].start()
+        to_side[0].wait_recv()
+        on_near.start()
+        relays[2].start()
+        to_near[1].wait_recv()
+        relays[1].start()
+        to_side[1].wait_recv()
+        relays[3].start()
+        from_side = copy(got[4], got[4], send.at[4], take.at[4], {"ctx": side})
+        from_near = copy(got[5], got[5], send.at[5], take.at[5], {"ctx": near})
+        from_side.wait_recv()
+        relays[4].start()
+        from_near.wait_recv()
+        relays[5].start()
+
+        def weights_from(k, carry):
+            member = lax.rem(me + groups - k, groups)
+            copy(
+                weights_ref.at[0], got_ref.at[member], put.at[k], away.at[member], place(member)
+            ).wait_recv()
+            return carry
+
+        lax.fori_loop(1, groups, weights_from, 0)
+
+        def weights_sent(k, carry):
+            peer = lax.rem(me + k, groups)
+            copy(
+                weights_ref.at[peer % ctxs], got_ref.at[me], put.at[k], away.at[me], place(peer)
+            ).wait_send()
+            return carry
+
+        lax.fori_loop(1, groups, weights_sent, 0)
+        for p in (0, 1):
+            to_near[p].wait_send()
+            to_side[p].wait_send()
+        on_side.wait_send()
+        on_near.wait_send()
+        mine.wait()
+        for passing in relays:
+            passing.wait()
+        for land in lands:
+            land.wait()
+
+    anywhere = pl.BlockSpec(memory_space=pl.ANY)
+    return pl.pallas_call(
+        body,
+        name="gather_rows",
+        out_shape=(
+            jax.ShapeDtypeStruct((ctxs, tps, half, width), BF16),
+            jax.ShapeDtypeStruct((groups,) + piece, BF16),
+        ),
+        in_specs=[anywhere] * 2,
+        out_specs=(anywhere, anywhere),
+        scratch_shapes=[
+            pltpu.VMEM((half, width), BF16),
+            pltpu.VMEM(piece, BF16),
+            pltpu.SemaphoreType.DMA((6,)),
+            pltpu.SemaphoreType.DMA((6,)),
+            pltpu.SemaphoreType.DMA((7,)),
+            pltpu.SemaphoreType.DMA((7,)),
+            pltpu.SemaphoreType.DMA((groups,)),
+            pltpu.SemaphoreType.DMA((groups,)),
+            pltpu.SemaphoreType.DMA((4,)),
+        ],
+        compiler_params=pltpu.CompilerParams(collective_id=collective_id, has_side_effects=True),
+    )(unit_half, weights)
 
 
 def nt(left, right):
@@ -401,7 +553,7 @@
     )(lengths, projected, projected, projected, mixed, grad_mixed, lse)
 
 
-def pair_sum(name, collective_id, partial):
+def pair_sum(collective_id, partial):
     shape = partial.shape[1:]
 
     def body(in_ref, out_ref, own, got, sems):
@@ -431,7 +583,6 @@
 
     return pl.pallas_call(
         body,
-        name=name,
         out_shape=jax.ShapeDtypeStruct(shape, BF16),
         in_specs=[pl.BlockSpec(memory_space=pl.ANY)],
         out_specs=pl.BlockSpec(memory_space=pltpu.VMEM),
@@ -557,12 +708,12 @@
 
 
 def home_kernel(
-    experts, limit, where_ref, cot_ref, middle_ref, second_ref, probs_ref, gate_ref, route_ref, target_ref,
+    limit, where_ref, cot_ref, middle_ref, second_ref, probs_ref, gate_ref, route_ref, target_ref,
     own_slot_ref, par_slot_ref, back_own_ref, back_par_ref, grad_ref, gain_ref, router_ref, proj_ref,
     output_ref, grad_middle_ref, grad_branch_ref, grad_mixed_ref, grad_logits_ref, grad_gain_ref,
 ):
     i = pl.program_id(0)
-    tile, width = cot_ref.shape
+    tile, _ = cot_ref.shape
     target = target_ref[...]
     pick_own = (target == own_slot_ref[...]).astype(F32).astype(BF16)
     pick_par = (target == par_slot_ref[...]).astype(F32).astype(BF16)
@@ -598,12 +749,15 @@
     grad_middle_ref[...] = grad_middle
     grad_branch = grad_middle.astype(BF16)
     grad_branch_ref[...] = grad_branch
-    grad_mixed_ref[...] = nn(grad_branch, proj_ref[...]).astype(BF16)
+    grad_mixed = nn(grad_branch, proj_ref[...]).astype(BF16)
+    ctxs, _, wide = grad_mixed_ref.shape
+    for c in range(ctxs):
+        grad_mixed_ref[c] = grad_mixed[:, c * wide : (c + 1) * wide]
 
 
 def home_step(
     cot, middle, second, probs, gate, route, target, own_slot, par_slot, back_own, back_par, grads,
-    gain, router, proj, where, experts, limit,
+    gain, router, proj, where, limit, ctxs,
 ):
     count, width = cot.shape
     features = proj.shape[1]
@@ -617,13 +771,13 @@
         return pl.BlockSpec(array.shape, lambda i, w: (0,) * array.ndim)
 
     return pl.pallas_call(
-        functools.partial(home_kernel, experts, limit),
+        functools.partial(home_kernel, limit),
         name="home_step",
         out_shape=(
             shape_of((count, width), BF16),
             shape_of((count, width), F32),
             shape_of((count, width), BF16),
-            shape_of((count, features), BF16),
+            shape_of((ctxs, count, features // ctxs), BF16),
             shape_of((count, pad), BF16),
             shape_of((1, width), F32),
         ),
@@ -636,7 +790,8 @@
                 whole(gain), whole(router), whole(proj),
             ],
             out_specs=[
-                rows(width), rows(width), rows(width), rows(features), rows(pad),
+                rows(width), rows(width), rows(width),
+                pl.BlockSpec((ctxs, tile, features // ctxs), lambda i, w: (0, i, 0)), rows(pad),
                 pl.BlockSpec((1, width), lambda i, w: (0, 0)),
             ],
         ),
@@ -672,6 +827,70 @@
         in_specs=[rows, rows, got, got, weight, weight],
         out_specs=rows,
     )(tokens, grad_middle, own, par, weight_own, weight_par)
+
+
+def expert_forward_kernel(rows_ref, w_in_ref, w_out_ref, hidden_ref, slope_ref, out_ref, total):
+    j = pl.program_id(0)
+    pre = nn(rows_ref[...], w_in_ref[...])
+    square = pre * pre
+    bend = jnp.tanh(pre * (GELU_A + (GELU_A * GELU_B) * square))
+    rise = 0.5 + 0.5 * bend
+    hidden = (pre * rise).astype(BF16)
+    hidden_ref[...] = hidden
+    slope = rise + (0.5 * pre) * (1.0 - bend * bend) * (GELU_A + (3.0 * GELU_A * GELU_B) * square)
+    slope_ref[...] = slope.astype(BF16)
+    part = nn(hidden, w_out_ref[...])
+
+    @pl.when(j == 0)
+    def _():
+        total[...] = part
+
+    @pl.when(j > 0)
+    def _():
+        total[...] += part
+
+    @pl.when(j == pl.num_programs(0) - 1)
+    def _():
+        out_ref[...] = total[...].astype(BF16)
+
+
+def expert_backward_kernel(grad_ref, slope_ref, w_in_ref, w_out_ref, grad_pre_ref, out_ref, total):
+    j = pl.program_id(0)
+    grad_pre = (nt(grad_ref[...], w_out_ref[...]) * slope_ref[...].astype(F32)).astype(BF16)
+    grad_pre_ref[...] = grad_pre
+    part = nt(grad_pre, w_in_ref[...])
+
+    @pl.when(j == 0)
+    def _():
+        total[...] = part
+
+    @pl.when(j > 0)
+    def _():
+        total[...] += part
+
+    @pl.when(j == pl.num_programs(0) - 1)
+    def _():
+        out_ref[...] = total[...].astype(BF16)
+
+
+UNITS = 256
+
+
+def expert_step(kernel, operands, w_in, w_out, results):
+    width, units = w_in.shape
+    count = operands[0].shape[0]
+    tile = min(UNITS, units)
+    whole = pl.BlockSpec((count, width), lambda j: (0, 0))
+    part = pl.BlockSpec((count, tile), lambda j: (0, j))
+    return pl.pallas_call(
+        kernel,
+        grid=(units // tile,),
+        out_shape=(shape_of((count, units), BF16),) * results + (shape_of((count, width), BF16),),
+        in_specs=[whole] + [part] * (len(operands) - 1)
+        + [pl.BlockSpec((width, tile), lambda j: (0, j)), pl.BlockSpec((tile, width), lambda j: (j, 0))],
+        out_specs=(part,) * results + (whole,),
+        scratch_shapes=[pltpu.VMEM((count, width), F32)],
+    )(*operands, w_in, w_out)
 
 
 def owner_kernel(shards, ctxs, wide, got_ref, weight_ref, gain_ref, grad_ref, sum_ref):
@@ -732,24 +951,7 @@
     unit_half, sent_weights, row_weights = prepare(
         rows_in, weight_qkv, small, tp_rank.astype(jnp.int32)[None], half, ctxs, wide, experts
     )
-    unit_all, got_weights = exchange(
-        "gather_rows", 1, sizes,
-        [
-            Item(
-                "ctx", unit_half, [shape_of((ctxs, tps, half, width), BF16)],
-                lambda ref, p: ref,
-                lambda ref, q, t: ref.at[q, t],
-                relay=lambda ref, q, t: ref.at[q, t],
-                block=(half, width),
-            ),
-            Item(
-                "all", sent_weights, [shape_of((groups, rows, 3 * wide + pad), BF16)],
-                lambda ref, p: ref.at[p % ctxs],
-                lambda ref, q, t: ref.at[q],
-                block=(rows, 3 * wide + pad),
-            ),
-        ],
-    )
+    unit_all, got_weights = gather_step(1, sizes, unit_half, sent_weights)
     unit_all, got_weights, row_weights, weight_late, routes, cot_late = lax.optimization_barrier(
         (unit_all, got_weights, row_weights, weight_proj, routes, cot)
     )
@@ -791,8 +993,8 @@
             lambda ref, p: ref, None, relay=lambda ref, q, t: ref, keep=False,
         )
 
-    mixed_own, mixed_par, proj_par, qkv_par = exchange(
-        "mixed_home", 2, sizes,
+    mixed_own, mixed_par, proj_par = exchange(
+        2, sizes,
         [
             Item(
                 "ctx", mixed_heads,
@@ -803,7 +1005,6 @@
                 block=(count, wide),
             ),
             passed(whole_proj),
-            passed(whole_qkv),
         ],
     )
 
@@ -830,7 +1031,7 @@
         )
 
     got_gates, got_rows, cot_par = exchange(
-        "dispatch", 3, sizes, [scattered(gate_rows), scattered(sent_rows), passed(got_cot)]
+        3, sizes, [scattered(gate_rows), scattered(sent_rows), passed(got_cot)]
     )
 
     slots_half = groups * half_cap
@@ -839,19 +1040,18 @@
     gates = got_gates[:, :, 0, :half_cap].reshape(total_rows)
     cot_rows = jnp.concatenate([got_cot, cot_par], axis=0).reshape(total_rows, width)
     grad_rows = (gates[:, None] * cot_rows.astype(F32)).astype(BF16)
-    pre = nn(arrived, w_in[0])
-    hidden, gelu_back = jax.vjp(jax.nn.gelu, pre)
-    hidden = hidden.astype(BF16)
-    partial_out = nn(hidden, w_out[0]).astype(BF16).reshape(tps, groups, half_cap, width)
-    summed = pair_sum("sum_out", 4, partial_out)
+    hidden, slope, partial_out = expert_step(
+        expert_forward_kernel, (arrived,), w_in[0], w_out[0], 2
+    )
+    summed = pair_sum(4, partial_out.reshape(tps, groups, half_cap, width))
     going_back = lax.all_to_all(summed, group, split_axis=0, concat_axis=0, tiled=True)
 
-    grad_hidden = nt(grad_rows, w_out[0])
-    grad_pre = gelu_back(grad_hidden)[0].astype(BF16)
-    partial_grad = nt(grad_pre, w_in[0]).astype(BF16).reshape(tps, groups, half_cap, width)
-    grad_summed = pair_sum("sum_grad", 5, partial_grad)
-    grad_home, back_par = exchange(
-        "grad_home", 6, sizes, [scattered(grad_summed), passed(going_back)]
+    grad_pre, partial_grad = expert_step(
+        expert_backward_kernel, (grad_rows, slope), w_in[0], w_out[0], 1
+    )
+    grad_summed = pair_sum(5, partial_grad.reshape(tps, groups, half_cap, width))
+    grad_home, back_par, qkv_par = exchange(
+        6, sizes, [scattered(grad_summed), passed(going_back), passed(whole_qkv)]
     )
 
     where = jnp.stack([ctx_rank * count, lengths[0]]).astype(jnp.int32)
@@ -859,17 +1059,17 @@
         cot, middle, second, probs, gate, route_column, target.reshape(count, 1),
         own_slot.reshape(1, slots_half), par_slot.reshape(1, slots_half),
         going_back.reshape(slots_half, width), back_par.reshape(slots_half, width),
-        grad_home.reshape(tps, slots_half, width), full_two, full_small, whole_proj, where, experts,
-        experts * capacity,
+        grad_home.reshape(tps, slots_half, width), full_two, full_small, whole_proj, where,
+        experts * capacity, ctxs,
     )
     output = output.reshape(slots, count, width)
 
     (grad_mixed,) = exchange(
-        "grad_mixed", 7, sizes,
+        7, sizes,
         [
             Item(
                 "ctx", grad_mixed_own, [shape_of((length_all, wide), BF16)],
-                lambda ref, p: ref.at[:, pl.ds(pl.multiple_of(p * wide, wide), wide)],
+                lambda ref, p: ref.at[p],
                 lambda ref, q, t: ref.at[pl.ds(pl.multiple_of(q * count, count), count), :],
                 block=(count, wide),
             ),
@@ -898,11 +1098,12 @@
         (unit_all, hidden, arrived, grad_rows, grad_pre, grad_projected)
     )
     grad_weight = tn(unit_late, grad_projected).astype(BF16).reshape(groups, rows, 3 * wide)
-    got_grad = lax.all_to_all(grad_weight, group, split_axis=0, concat_axis=0, tiled=True)
     grad_w_out = tn(hidden, grad_rows)[None]
     grad_w_in = tn(arrived, grad_pre)[None]
-
-    (grad_par,) = exchange("grad_pair", 8, sizes, [passed(grad_own)])
+    grad_weight, grad_own = lax.optimization_barrier((grad_weight, grad_own))
+    got_grad = lax.all_to_all(grad_weight, group, split_axis=0, concat_axis=0, tiled=True)
+
+    (grad_par,) = exchange(8, sizes, [passed(grad_own)])
     grad_tokens = last_step(rows_in, grad_middle, grad_own, grad_par, whole_qkv, qkv_par)
     grad_tokens = grad_tokens.reshape(slots, count, width)
     owned_qkv, sums = owner_step(got_grad, weight_qkv, gain_one.reshape(rows, 1), shards, ctxs, wide)

time: 632 us -> 577 us (0.913)
  Pallas kernels: 295 us -> 394 us
  waiting for transfers between devices: 111 us -> 37.7 us
  blocking collectives: 62.2 us -> 2.97 us
  matrix products: 94.2 us -> 51.1 us
  starting transfers between devices: 23.1 us -> 45.9 us
    all_gather x1, waiting for transfers between devices: 70.1 us -> 0.02 us  [local(): whole_qkv = lax.all_gather(row_weights, group, axis=0, tiled=True)]
    pallas_call x9 -> x11, Pallas kernels: 192 us -> 261 us  [the longest x5 102 us: exchange(): pl.pallas_call(body, out_shape=tuple(out_shapes), in_specs=[anywhere] * l...]
    all_to_all x1 -> x0, blocking collectives: 59.2 us -> none  [local(): lax.all_to_all(grad_weight, group, split_axis=0, concat_axis=0, tiled=True)]
    dot_general x2 -> x0, matrix products: 25.3 us -> none  [nt(): lax.dot_general(left, right, (((1,), (1,)), ((), ())), preferred_element_...]
    dot_general x6 -> x4, matrix products: 37 us -> 16.5 us  [nn(): lax.dot_general(left, right, (((1,), (0,)), ((), ())), preferred_element_...]
    pallas_call x1, Pallas kernels: 42.7 us -> 63.1 us  [attention_backward(): pl.pallas_call(functools.partial(backward_kernel, heads, size, blocks), n...]
    all_to_all x1, starting transfers between devices: 15.2 us -> 30.9 us  [local(): lax.all_to_all(summed, group, split_axis=0, concat_axis=0, tiled=True)]
    pallas_call x1, Pallas kernels: 30.7 us -> 40.7 us  [attention_forward(): pl.pallas_call(functools.partial(forward_kernel, heads, size, span, count...]
  transfers between devices with their start and end apart: 6 -> 7, of which waited for: 3 -> 2; matrix products, arithmetic and copies ran while one was open for 14% -> 11% of each run, Pallas kernels for 13% -> 47%
where the time goes in v3:
time: 577 us; the launch traced here: 573 us
  Pallas kernels  394 us (68%)
  matrix products  51.1 us (9%)
  starting transfers between devices  45.9 us (8%)
  waiting for transfers between devices  37.7 us (7%)
  local copies, waits for them, and re-layouts  16.9 us (3%)
  between operations  15 us (3%)
  other arithmetic  9.41 us (2%)
    pallas_call x5, Pallas kernels, exchange(): pl.pallas_call(body, out_shape=tuple(out_shapes), in_specs=[anywhere] * l...  102 us
    pallas_call x2, Pallas kernels, expert_step(): pl.pallas_call(kernel, grid=(units // tile,), out_shape=(shape_of((count,...  75.4 us
    pallas_call x1, Pallas kernels, attention_backward(): pl.pallas_call(functools.partial(backward_kernel, heads, size, blocks), n...  63.1 us
    pallas_call x1, Pallas kernels, gather_step(): pl.pallas_call(body, name='gather_rows', out_shape=(jax.ShapeDtypeStruct(...  56.4 us
    pallas_call x1, Pallas kernels, attention_forward(): pl.pallas_call(functools.partial(forward_kernel, heads, size, span, count...  40.7 us
    dot_general x5, matrix products, tn(): lax.dot_general(left, right, (((0,), (0,)), ((), ())), preferred_element_...  34.6 us
    all_to_all x1, waiting for transfers between devices, local(): lax.all_to_all(grad_projected.reshape(ctxs, count, 3 * wide), 'ctx', spli...  34.4 us
    all_to_all x1, starting transfers between devices, local(): lax.all_to_all(summed, group, split_axis=0, concat_axis=0, tiled=True)  30.9 us
  transfers between devices with their start and end apart: 7, of which 2 were waited for; matrix products, arithmetic and copies ran while one was open for 11% of the time, Pallas kernels for 47%

profile of v3, /device:TPU:0, one launch (start us, length us, event | category | flops | bytes accessed | tf_op | source)
XLA Modules:
  0.0 572.8 jit_solution(1832440448700827323)
XLA Ops:
  10.5 3.1 prepare.1
  13.6 56.4 %gather_rows.1 = (bf16[4,2,512,1024]{3,2,1,0:T(8,128)(2,1)}, bf16[16,64,512]{2,1,0:T(8,128)(2,1)}) custom-call(bf16[512,1024]{1,0:T(8,128)(2,1)} %get-tuple-element.56.rows_ref, bf16[4,64,512]{2,1,0:T(8,128)(2,1)} %get-tuple-element.57.weights_ref), custom_call_target="tpu_custom_call" | custom-call | tf_op jit(solution)/shard_map/gather_rows/pallas_call | solution.py:313
  71.2 2.6 fusion.10
  73.9 3.8 all-to-all-start
  79.4 9.1 %convolution_convert_fusion.q_ref.k_ref.v_ref = bf16[4096,384]{1,0:T(8,128)(2,1)} fusion(bf16[4096,1024]{1,0:T(8,128)(2,1)} %bitcast.82, bf16[1024,512]{1,0:T(8,128)(2,1)S(1)} %bitcast.73), kind=kOutput, calls=%fused_computation | convolution fusion | flops 3222798336 | bytes 12320768 | tf_op jit(solution)/shard_map/dot_general | solution.py:342
  90.2 40.7 %attention_forward.1 = (bf16[4096,128]{1,0:T(8,128)(2,1)}, f32[8,1,1024]{2,1,0:T(1,128)}) custom-call(s32[1]{0:T(128)} %copy.60.len_ref, bf16[4096,384]{1,0:T(8,128)(2,1)} %convolution_convert_fusion.q_ref.k_ref.v_ref, bf16[4096,384]{1,0:T(8,128)(2,1)} %convolution_convert_fusion.q_ref.k_ref.v_ref, bf16[4096,384]{1,0:T(8,128)(2,1)} %convolution_convert_fusion.q_ref.k_ref.v_ref), custom_call_target="tpu_custom_call" | custom-call | flops 34359738368 | bytes 4194304 | tf_op jit(solution)/shard_map/attention_forward/pallas_call | solution.py:416
  130.9 2.9 all-gather.3.cloned.1.call-done.refs_1_.proj_own_ref.proj_ref
  133.8 17.9 %shard_map.178 = (bf16[1024,512]{1,0:T(8,128)(2,1)}, bf16[1024,512]{1,0:T(8,128)(2,1)}, bf16[1024,512]{1,0:T(8,128)(2,1)}) custom-call(bf16[4096,128]{1,0:T(8,128)(2,1)} %get-tuple-element.63.refs_0_.o_ref, bf16[1024,512]{1,0:T(8,128)(2,1)} %all-gather.3.cloned.1.call-done.refs_1_.proj_own_ref.proj_ref), custom_call_target="tpu_custom_call" | custom-call | tf_op jit(solution)/shard_map/pallas_call | solution.py:175
  151.7 8.9 %middle_step.1 = (f32[1024,1024]{1,0:T(8,128)}, bf16[1024,1024]{1,0:T(8,128)(2,1)}, f32[1024,128]{1,0:T(8,128)}, f32[1024,1]{1,0:T(8,128)}) custom-call(bf16[1024,1024]{1,0:T(8,128)(2,1)} %bitcast.52, bf16[1024,512]{1,0:T(8,128)(2,1)} %get-tuple-element.65.own_ref, bf16[1024,512]{1,0:T(8,128)(2,1)} %get-tuple-element.66.par_ref, ...), custom_call_target="tpu_custom_call" | custom-call | tf_op jit(solution)/shard_map/middle_step/pallas_call | solution.py:692
  162.5 4.2 fusion.7
  167.8 30.2 %shard_map.179 = (f32[2,16,8,128]{3,2,1,0:T(8,128)}, bf16[2,16,40,1024]{3,2,1,0:T(8,128)(2,1)}, bf16[16,40,1024]{2,1,0:T(8,128)(2,1)}) custom-call(f32[16,8,128]{2,1,0:T(8,128)} %broadcast_in_dim.62.refs_0_, bf16[16,40,1024]{2,1,0:T(8,128)(2,1)} %bitcast.69, bf16[16,40,1024]{2,1,0:T(8,128)(2,1)} %copy-done.2), custom_call_target="tpu_custom_call" | custom-call | tf_op jit(solution)/shard_map/pallas_call | solution.py:175
  198.0 45.2 %shard_map.180 = (bf16[1280,2048]{1,0:T(8,128)(2,1)}, bf16[1280,2048]{1,0:T(8,128)(2,1)}, bf16[1280,1024]{1,0:T(8,128)(2,1)}) custom-call(bf16[1280,1024]{1,0:T(8,128)(2,1)} %bitcast.64, bf16[1024,2048]{1,0:T(8,128)(2,1)} %bitcast.54, bf16[2048,1024]{1,0:T(8,128)(2,1)} %bitcast.56), custom_call_target="tpu_custom_call" | custom-call | tf_op jit(solution)/shard_map/pallas_call | solution.py:885
  243.2 4.7 shard_map.181
  248.0 30.9 %all-to-all-start.1 = ((bf16[16,40,1024]{2,1,0:T(8,128)(2,1)}), bf16[16,40,1024]{2,1,0:T(8,128)(2,1)S(1)}, u32[]{:S(2)}, u32[]{:S(2)}) async-start(bf16[16,40,1024]{2,1,0:T(8,128)(2,1)} %shard_map.181), calls=%async_computation.1 | async-start | bytes 2621440 | tf_op jit(solution)/shard_map/all_to_all | solution.py:1047
  287.8 30.1 %shard_map.182 = (bf16[1280,2048]{1,0:T(8,128)(2,1)}, bf16[1280,1024]{1,0:T(8,128)(2,1)}) custom-call(bf16[1280,1024]{1,0:T(8,128)(2,1)} %fusion.grad_ref, bf16[1280,2048]{1,0:T(8,128)(2,1)} %get-tuple-element.78.slope_ref, bf16[1024,2048]{1,0:T(8,128)(2,1)} %bitcast.55, bf16[2048,1024]{1,0:T(8,128)(2,1)} %bitcast.57), custom_call_target="tpu_custom_call" | custom-call | tf_op jit(solution)/shard_map/pallas_call | solution.py:885
  317.9 4.7 shard_map.183.refs_0_
  323.7 28.0 %shard_map.184 = (bf16[2,16,40,1024]{3,2,1,0:T(8,128)(2,1)}, bf16[16,40,1024]{2,1,0:T(8,128)(2,1)}, bf16[1024,1536]{1,0:T(8,128)(2,1)}) custom-call(bf16[16,40,1024]{2,1,0:T(8,128)(2,1)} %shard_map.183.refs_0_, bf16[16,40,1024]{2,1,0:T(8,128)(2,1)} %copy-done.1, bf16[1024,1536]{1,0:T(8,128)(2,1)} %all-gather.5.cloned.1.call-done.refs_2_.weight_own_ref), custom_call_target="tpu_custom_call" | custom-call | tf_op jit(solution)/shard_map/pallas_call | solution.py:175
  351.8 17.7 %home_step.1 = (bf16[1024,1024]{1,0:T(8,128)(2,1)}, f32[1024,1024]{1,0:T(8,128)}, bf16[1024,1024]{1,0:T(8,128)(2,1)}, bf16[4,1024,128]{2,1,0:T(8,128)(2,1)}, bf1...) custom-call(s32[2]{0:T(128)} %pad_add_fusion.where_ref, bf16[1024,1024]{1,0:T(8,128)(2,1)} %bitcast.66, ...), custom_call_target="tpu_custom_call" | custom-call | tf_op jit(solution)/shard_map/home_step/pallas_call | solution.py:773
  369.5 19.6 %shard_map.185.do_ref = bf16[4096,128]{1,0:T(8,128)(2,1)} custom-call(bf16[4,1024,128]{2,1,0:T(8,128)(2,1)} %get-tuple-element.87.refs_0_), custom_call_target="tpu_custom_call" | custom-call | tf_op jit(solution)/shard_map/pallas_call | solution.py:175
  389.1 3.0 fusion.40
  392.9 2.1 copy.55
  394.9 63.1 %attention_backward.1 = bf16[4096,384]{1,0:T(8,128)(2,1)} custom-call(s32[1]{0:T(128)} %copy.60.len_ref, bf16[4096,384]{1,0:T(8,128)(2,1)} %convolution_convert_fusion.q_ref.k_ref.v_ref, bf16[4096,384]{1,0:T(8,128)(2,1)} %convolution_convert_fusion.q_ref.k_ref.v_ref, bf16[4096,384]{1,0:T(8,128)(2,1)} %convolution_convert_fusion.q_ref.k_ref.v_ref, ...), custom_call_target="tpu_custom_call" | custom-call | flops 85899345920 | bytes 8388608 | tf_op jit(solution)/shard_map/attention_backward/pallas_call | solution.py:525
  458.0 3.9 all-to-all-start.2
  461.9 9.8 %convolution_convert_fusion.1 = bf16[1024,384]{1,0:T(8,128)(2,1)} fusion(bf16[4096,1024]{1,0:T(8,128)(2,1)} %bitcast.83, bf16[4096,384]{1,0:T(8,128)(2,1)} %attention_backward.1), kind=kOutput, calls=%fused_computation.17 | convolution fusion | flops 3221618688 | bytes 12320768 | tf_op jit(solution)/shard_map/dot_general | solution.py:346
  471.7 34.4 %all-to-all-done.2.refs_0_.own_ref = bf16[4,1024,384]{2,1,0:T(8,128)(2,1)S(1)} async-done(((bf16[4,1024,384]{2,1,0:T(8,128)(2,1)}), bf16[4,1024,384]{2,1,0:T(8,128)(2,1)S(1)}, u32[]{:S(2)}, u32[]{:S(2)}) %all-to-all-start.2) | async-done | bytes 3145760 | tf_op jit(solution)/shard_map/all_to_all | solution.py:1093
  506.1 6.8 %all-to-all-start.3 = ((bf16[16,64,384]{2,1,0:T(8,128)(2,1)}), bf16[16,64,384]{2,1,0:T(8,128)(2,1)}, u32[]{:S(2)}, u32[]{:S(2)}) async-start(bf16[16,64,384]{2,1,0:T(8,128)(2,1)} %bitcast.70), calls=%async_computation.3 | async-start | bytes 1572864 | tf_op jit(solution)/shard_map/all_to_all | solution.py:1104
  512.9 10.9 %convolution_bitcast_fusion = f32[1,2048,1024]{2,1,0:T(8,128)} fusion(bf16[1280,2048]{1,0:T(8,128)(2,1)} %get-tuple-element.101, bf16[1280,1024]{1,0:T(8,128)(2,1)} %fusion.grad_ref), kind=kOutput, calls=%fused_computation.3 | convolution fusion | flops 5368709120 | bytes 16252928 | tf_op jit(solution)/shard_map/dot_general | solution.py:346
  523.8 10.4 %convolution_bitcast_fusion.1 = f32[1,1024,2048]{2,1,0:T(8,128)} fusion(bf16[1280,1024]{1,0:T(8,128)(2,1)S(1)} %bitcast.65, bf16[1280,2048]{1,0:T(8,128)(2,1)} %get-tuple-element.100), kind=kOutput, calls=%fused_computation.4 | convolution fusion | flops 5368709120 | bytes 16252928 | tf_op jit(solution)/shard_map/dot_general | solution.py:346
  534.2 6.1 %shard_map.186.par_ref = bf16[4,1024,384]{2,1,0:T(8,128)(2,1)} custom-call(bf16[4,1024,384]{2,1,0:T(8,128)(2,1)} %copy-done), custom_call_target="tpu_custom_call" | custom-call | tf_op jit(solution)/shard_map/pallas_call | solution.py:175
  540.3 15.3 %last_step.1 = f32[1024,1024]{1,0:T(8,128)} custom-call(bf16[1024,1024]{1,0:T(8,128)(2,1)} %bitcast.53, f32[1024,1024]{1,0:T(8,128)} %get-tuple-element.84.grad_middle_ref, bf16[4,1024,384]{2,1,0:T(8,128)(2,1)} %copy-done, bf16[4,1024,384]{2,1,0:T(8,128)(2,1)} %shard_map.186.par_ref, bf16[1024,1536]{1,0:T(8,128)(2,1)} %all-gather.5.cloned.1.call-done.refs_2_.weight_own_ref, ...), custom_call_target="tpu_custom_call" | custom-call | tf_op jit(solution)/shard_map/last_step/pallas_call | solution.py:822
  555.6 2.1 owner_step.1
  558.6 3.0 psum.7
  (77 shorter events, 26.0 us)
Async XLA Ops:
  7.2 64.0 %copy-start.7 = (bf16[1,1024,1024]{2,1,0:T(8,128)(2,1)S(1)}, bf16[1,1024,1024]{2,1,0:T(8,128)(2,1)}, u32[]{:S(2)}) copy-start(bf16[1,1024,1024]{2,1,0:T(8,128)(2,1)} %param.21) | copy-start | bytes 6291460
  7.2 63.5 %copy-start.12 = (s32[1,1024,1]{1,2,0:T(1,128)S(1)}, s32[1,1024,1]{1,2,0:T(1,128)}, u32[]{:S(2)}) copy-start(s32[1,1024,1]{1,2,0:T(1,128)} %param.13) | copy-start | bytes 12292
  7.2 126.6 %all-gather.3.cloned.1.call-start = ((), (), s32[]{:S(2)}) async-start(), calls=%async_computation.5 | async-start | bytes 1114112 | tf_op jit(solution)/shard_map/all_gather | solution.py:959
  8.1 63.1 %copy-start.11 = (bf16[64,1]{1,0:T(8,128)(2,1)}, bf16[64,1]{1,0:T(8,128)(2,1)S(1)}, u32[]{:S(2)}) copy-start(bf16[64,1]{1,0:T(8,128)(2,1)S(1)} %copy.47.gain_ref) | copy-start | bytes 388
  73.9 4.6 copy-start.10
  73.9 92.8 %all-to-all-start = ((bf16[16,40,1024]{2,1,0:T(8,128)(2,1)}), bf16[16,40,1024]{2,1,0:T(8,128)(2,1)S(1)}, u32[]{:S(2)}, u32[]{:S(2)}) async-start(bf16[16,40,1024]{2,1,0:T(8,128)(2,1)} %bitcast.13), calls=%async_computation | async-start | bytes 2621440 | tf_op jit(solution)/shard_map/all_to_all | solution.py:985
  77.7 245.0 %all-gather.5.cloned.1.call-start = ((), (), s32[]{:S(2)}) async-start(), calls=%async_computation.6 | async-start | bytes 3342336 | tf_op jit(solution)/shard_map/all_gather | solution.py:958
  166.7 1.1 copy-start.2
  243.2 38.1 %copy-start.5 = (s32[1024,1]{1,0:T(8,128)S(1)}, s32[1024,1]{1,0:T(8,128)}, u32[]{:S(2)}) copy-start(s32[1024,1]{1,0:T(8,128)} %copy.48.route_ref) | copy-start | bytes 12292
  248.0 36.3 %copy-start.3 = (bf16[16,40,1024]{2,1,0:T(8,128)(2,1)S(1)}, bf16[16,40,1024]{2,1,0:T(8,128)(2,1)}, u32[]{:S(2)}) copy-start(bf16[16,40,1024]{2,1,0:T(8,128)(2,1)} %copy-done.2) | copy-start | bytes 3932164
  248.0 74.7 %all-to-all-start.1 = ((bf16[16,40,1024]{2,1,0:T(8,128)(2,1)}), bf16[16,40,1024]{2,1,0:T(8,128)(2,1)S(1)}, u32[]{:S(2)}, u32[]{:S(2)}) async-start(bf16[16,40,1024]{2,1,0:T(8,128)(2,1)} %shard_map.181), calls=%async_computation.1 | async-start | bytes 2621440 | tf_op jit(solution)/shard_map/all_to_all | solution.py:1047
  278.9 282.7 %reduce-scatter.4.cloned.1.call-start = ((), (), s32[]{:S(2)}) async-start(), calls=%async_computation.7 | async-start | bytes 2785280
  322.7 1.1 copy-start.1
  351.8 37.3 %copy-start.8 = (bf16[1024,512]{1,0:T(8,128)(2,1)S(1)}, bf16[1024,512]{1,0:T(8,128)(2,1)}, u32[]{:S(2)}) copy-start(bf16[1024,512]{1,0:T(8,128)(2,1)} %get-tuple-element.65.own_ref) | copy-start | bytes 3145732
  389.1 3.1 copy-start.4
  389.1 3.1 copy-start.9
  389.1 3.5 copy-start.13
  458.0 48.0 %all-to-all-start.2 = ((bf16[4,1024,384]{2,1,0:T(8,128)(2,1)}), bf16[4,1024,384]{2,1,0:T(8,128)(2,1)S(1)}, u32[]{:S(2)}, u32[]{:S(2)}) async-start(bf16[4,1024,384]{2,1,0:T(8,128)(2,1)} %bitcast.60), calls=%async_computation.2 | async-start | bytes 6291456 | tf_op jit(solution)/shard_map/all_to_all | solution.py:1093
  506.1 17.7 %copy-start = (bf16[4,1024,384]{2,1,0:T(8,128)(2,1)}, bf16[4,1024,384]{2,1,0:T(8,128)(2,1)S(1)}, u32[]{:S(2)}) copy-start(bf16[4,1024,384]{2,1,0:T(8,128)(2,1)S(1)} %all-to-all-done.2.refs_0_.own_ref) | copy-start | bytes 9437188
  506.1 49.6 %all-to-all-start.3 = ((bf16[16,64,384]{2,1,0:T(8,128)(2,1)}), bf16[16,64,384]{2,1,0:T(8,128)(2,1)}, u32[]{:S(2)}, u32[]{:S(2)}) async-start(bf16[16,64,384]{2,1,0:T(8,128)(2,1)} %bitcast.70), calls=%async_computation.3 | async-start | bytes 1572864 | tf_op jit(solution)/shard_map/all_to_all | solution.py:1104
  512.9 10.9 %copy-start.6 = (bf16[2,16,40,1024]{3,2,1,0:T(8,128)(2,1)S(1)}, bf16[2,16,40,1024]{3,2,1,0:T(8,128)(2,1)}, u32[]{:S(2)}) copy-start(bf16[2,16,40,1024]{3,2,1,0:T(8,128)(2,1)} %get-tuple-element.74) | copy-start | bytes 7864324
Sparse Core Ops, SparseCore 0:
  70.1 63.6 all-gather.2
  136.6 86.3 all-gather.4
  395.1 91.2 reduce-scatter.3
